TPU v7x, 32 devices: a whole 2x2x4 slice. The times are simulated.
32 devices in a mesh: chain: 4 (over y, x), op: 8 (over z, core).
Axes of the slice: x: 2, y: 2, z: 4, core: 2. Of those that a mesh axis runs over, the one named last changes fastest.
Arguments:
- env_in: bfloat16 [16, 16, 128, 128], P('op'), may hold values from -6 to 6
- mps: bfloat16 [4, 4, 16, 128, 128], P('chain'), may hold values from -0.5 to 0.5
- proj: bfloat16 [4, 4, 16, 128, 128], P('chain'), may hold values from -0.5 to 0.5
- mpo: bfloat16 [4, 16, 4, 16, 4], P('chain'), may hold values from -2 to 2
- mpo_charge: int32 [16, 2], replicated, may hold values from -1 to 1
- block_sizes: int32 [5, 16], replicated, may hold values from 32 to 128
Outputs:
- env_out: bfloat16 [4, 16, 16, 128, 128], P('chain', 'op')
All inputs are finite; a program needn't handle non-finite values.
Results may differ from a plain program's by a relative error of at most 0.025.
Values may be sent and summed in bfloat16 or wider, within the bound.
No kernel may reach another device: no remote copies, remote signals or barrier semaphores. Data moves between devices by JAX's collectives and lax.ppermute only.
A program may use at most 64 MiB of HBM per device.

v0:
```python
import functools

import jax
import jax.numpy as jnp
from jax import lax
from jax.experimental import pallas as pl
from jax.experimental.pallas import tpu as pltpu
from jax.sharding import PartitionSpec as P


UP_VALUES = 8
DOWN_VALUES = 2
PHYS = 4

UP_CHARGE = (0, 1, 0, 1)
DOWN_CHARGE = (0, 0, 1, 1)

STATE_ORDER = (0, 2, 1, 3)
MPS_PARTS = ((0, 0, 2), (2, 0, 1), (1, -1, 2), (3, -1, 1))
MPS_BLOCKS = ((0, 0, 0), (0, 0, 1), (2, 0, 0), (1, -1, 0), (1, -1, 1), (3, -1, 0))
ROW_SHIFTS = 3
PROJ_PARTS = ((0, -1, 2), (1, -2, 2), (2, -1, 1), (3, -2, 1))
GROUP = 8


VMEM = pl.BlockSpec(memory_space=pltpu.VMEM)
SMEM = pl.BlockSpec(memory_space=pltpu.SMEM)
ANY = pl.BlockSpec(memory_space=pl.ANY)
HBM = pl.BlockSpec(memory_space=pltpu.HBM)


def ring_chain(position, count):
    turned = (position + count - 1) % count
    return turned ^ (turned >> 1)


def place(chain, count):
    plain = chain ^ (chain >> 1) ^ (chain >> 2)
    return (plain + 1) % count if isinstance(chain, int) else lax.rem(plain + 1, count)


def my_row(chain_count, spread):
    side = lax.rem(lax.axis_index("op"), spread)
    return place(lax.axis_index("chain"), chain_count) * spread + side


def held_rows(spread):
    return -(-(ROW_SHIFTS + spread - 1) // spread)


def held_base(first_row, offset, holder, spread):
    rows = held_rows(spread)
    return jnp.clip(first_row + offset + holder * rows, 0, UP_VALUES - rows)


def proj_start(phys_state, spread):
    start = len(MPS_BLOCKS)
    for part_state, _, downs in PROJ_PARTS:
        if part_state == phys_state:
            return start
        start += held_rows(spread) * downs
    return start


def mpo_matrix(site_mpo):
    bond = site_mpo.shape[0]
    ordered = jnp.stack([site_mpo[:, state] for state in STATE_ORDER], axis=1)
    return jnp.transpose(ordered, (2, 3, 1, 0)).reshape(bond * PHYS, PHYS * bond)


def call(kernel, *args, **options):
    return plain_call(kernel, *args, **options)


def plain_call(kernel, out_shape, specs, operands, scratch=(), limit=20, flops=10**8, place_out=VMEM):
    one = not isinstance(out_shape, (list, tuple))
    return pl.pallas_call(
        kernel,
        out_shape=out_shape,
        in_specs=specs,
        out_specs=place_out if one else tuple(place_out for _ in out_shape),
        scratch_shapes=list(scratch),
        compiler_params=pltpu.CompilerParams(vmem_limit_bytes=limit << 20),
        cost_estimate=pl.CostEstimate(flops=flops, bytes_accessed=10**6, transcendentals=0),
    )(*operands)


def shape_of(*dims, dtype=jnp.bfloat16):
    return jax.ShapeDtypeStruct(dims, dtype)


def run_copies(copies):
    for copy in copies:
        copy.start()
    for copy in copies:
        copy.wait()


def pack_env_kernel(chain_count, spread, env_ref, out_ref, sem):
    first = place(lax.axis_index("chain"), chain_count) * spread
    before = jnp.maximum(first - 1, 0)
    copies = []

    def add(source, target):
        copies.append(pltpu.make_async_copy(source, target, sem.at[len(copies)]))

    for bond in range(env_ref.shape[0]):
        add(env_ref.at[bond, pl.ds(before, 1)], out_ref.at[bond, pl.ds(0, 1)])
        add(env_ref.at[bond, pl.ds(first, spread)], out_ref.at[bond, pl.ds(1, spread)])
    run_copies(copies)


def pack_site_kernel(chain_count, spread, first_hop, mps_ref, proj_ref, *refs):
    out_refs, sem = refs[:-1], refs[-1]
    chain_pos = lax.axis_index("chain")
    side = lax.rem(lax.axis_index("op"), spread)
    is_last = (chain_pos == chain_count - 1).astype(jnp.int32)
    copies = []

    def add(source, target):
        copies.append(pltpu.make_async_copy(source, target, sem.at[len(copies)]))

    rows = held_rows(spread)
    for hop, out_ref in enumerate(out_refs, first_hop):
        first = place(jnp.bitwise_xor(chain_pos, hop), chain_count) * spread
        start = 0
        for phys_state, offset, downs in MPS_PARTS:
            late = is_last if offset else 0
            sector = jnp.maximum(first + side + offset + late, 0) * DOWN_VALUES
            add(
                mps_ref.at[0, phys_state, pl.ds(sector, downs)],
                out_ref.at[pl.ds(start, downs)],
            )
            start += downs
        for phys_state, offset, downs in PROJ_PARTS:
            base = held_base(first, offset, side, spread)
            start = proj_start(phys_state, spread)
            for down in range(downs):
                add(
                    proj_ref.at[0, phys_state, pl.ds(base, rows), down],
                    out_ref.at[pl.ds(start + down * rows, rows)],
                )
    run_copies(copies)


def pick_extra_kernel(last_site, chain_count, spread, *refs):
    weight_refs, out_ref, sem = refs[:-2], refs[-2], refs[-1]
    chain_pos = lax.axis_index("chain")
    slot = jnp.bitwise_xor(chain_pos, last_site)
    first = place(chain_pos, chain_count) * spread
    held = held_rows(spread)
    holder = (ROW_SHIFTS - 1) // held
    for index, weight_ref in enumerate(weight_refs):
        @pl.when(slot == index)
        def _():
            copies = []
            for phys_state, offset, downs in PROJ_PARTS:
                base = held_base(first, offset, holder, spread)
                at = jnp.clip(first + offset + ROW_SHIFTS - 1 - base, 0, held - 1)
                for down in range(downs):
                    copies.append(
                        pltpu.make_async_copy(
                            weight_ref.at[proj_start(phys_state, spread) + down * held + at],
                            out_ref.at[len(copies)],
                            sem.at[len(copies)],
                        )
                    )
            run_copies(copies)


def mask_kernel(charges, out_ref):
    rows, lanes = out_ref.shape
    bond = rows // PHYS
    row_at = lax.broadcasted_iota(jnp.int32, (rows, lanes), 0)
    lane_at = lax.broadcasted_iota(jnp.int32, (rows, lanes), 1)
    ones = jnp.ones((rows, lanes), jnp.float32)
    for axis, table in enumerate((UP_CHARGE, DOWN_CHARGE)):
        left = jnp.zeros((rows, lanes), jnp.int32)
        right = jnp.zeros((rows, lanes), jnp.int32)
        for index in range(bond):
            value = charges[index, axis]
            left = jnp.where(row_at // PHYS == index, value, left)
            right = jnp.where(lane_at % bond == index, value, right)
        for index in range(PHYS):
            left = left - jnp.where(row_at % PHYS == index, table[index], 0)
            right = right - jnp.where(lane_at // bond == index, table[STATE_ORDER[index]], 0)
        ones = jnp.where(left == right, ones, 0.0)
    out_ref[...] = ones


def turn_blocks(turned, row, side, spread, block, read, read_extra=None):
    held = held_rows(spread)
    turned[...] = jnp.zeros_like(turned)
    extra = 0
    for phys_state, offset, downs in PROJ_PARTS:
        for shift in range(ROW_SHIFTS):
            for target in range(DOWN_VALUES):
                down = target - DOWN_CHARGE[phys_state]
                if down < 0:
                    continue
                wanted = row + offset + shift
                holder = jnp.minimum((side + shift) // held, spread - 1)
                base = held_base(row - side, offset, holder, spread)
                at = jnp.clip(wanted - base, 0, held - 1)
                value = read(holder, proj_start(phys_state, spread) + down * held + at)
                if read_extra is not None and shift == ROW_SHIFTS - 1:
                    beyond = side + shift >= spread + ROW_SHIFTS - 1
                    value = jnp.where(beyond, read_extra(extra + down), value)
                inside = (wanted >= 0) & (wanted < UP_VALUES)
                turned[
                    shift * DOWN_VALUES + target,
                    :,
                    phys_state * block : (phys_state + 1) * block,
                ] = jnp.where(inside, value.T, jnp.zeros_like(value))
        extra += downs


def prep_kernel(site, last, chain_count, spread, bond, block, slots, sizes, mask, *refs):
    matrix_refs, refs = refs[:slots], refs[slots:]
    weight_refs, refs = refs[: slots * spread], refs[slots * spread :]
    extra_ref, refs = (refs[0], refs[1:]) if last else (None, refs)
    mps_ref, turned, kron = refs[:3]
    weights, sem = refs[-2:]
    row = my_row(chain_count, spread)
    side = lax.rem(lax.axis_index("op"), spread)
    slot = jnp.bitwise_xor(lax.axis_index("chain"), site)
    for index in range(slots):
        @pl.when(slot == index)
        def _():
            run_copies(
                [
                    pltpu.make_async_copy(
                        weight_refs[index * spread + turn],
                        weights.at[jnp.bitwise_xor(side, turn)],
                        sem.at[turn],
                    )
                    for turn in range(spread)
                ]
            )

    row_at = lax.broadcasted_iota(jnp.int32, (block, block), 0)
    column_at = lax.broadcasted_iota(jnp.int32, (block, block), 1)
    for index, (phys_state, offset, down) in enumerate(MPS_BLOCKS):
        late = 1 if last and offset else 0
        source = row + offset + late
        target = jnp.minimum(row + late, UP_VALUES - 1)
        high = sizes[site, jnp.maximum(source, 0) * DOWN_VALUES + down]
        wide = sizes[site + 1, target * DOWN_VALUES + down + DOWN_CHARGE[phys_state]]
        keep = (row_at < jnp.where(source >= 0, high, 0)) & (column_at < wide)
        value = weights[side, index]
        mps_ref[index] = jnp.where(keep, value, jnp.zeros_like(value))

    def read(holder, at):
        return weights[holder, at]

    turn_blocks(turned, row, side, spread, block, read)
    if last:

        turn_blocks(refs[3], row + 1, side + 1, spread, block, read, lambda at: extra_ref[at])

    pairs = bond * PHYS
    wide = pairs * GROUP
    matrix = matrix_refs[0][...].astype(jnp.float32)
    for index in range(1, slots):
        matrix = jnp.where(slot == index, matrix_refs[index][...].astype(jnp.float32), matrix)
    matrix = jnp.where(mask[...] > 0.5, matrix, 0.0).astype(jnp.bfloat16)
    lanes = matrix.shape[1]
    tall = (
        lax.broadcasted_iota(jnp.int32, (wide, pairs), 0) // GROUP
        == lax.broadcasted_iota(jnp.int32, (wide, pairs), 1)
    ).astype(jnp.bfloat16)
    across = (
        lax.broadcasted_iota(jnp.int32, (lanes, wide), 0)
        == lax.broadcasted_iota(jnp.int32, (lanes, wide), 1) // GROUP
    ).astype(jnp.bfloat16)
    spread_out = jnp.dot(tall, matrix, preferred_element_type=jnp.float32).astype(jnp.bfloat16)
    spread_out = jnp.dot(spread_out, across, preferred_element_type=jnp.float32)
    same = (
        lax.broadcasted_iota(jnp.int32, (wide, wide), 0) % GROUP
        == lax.broadcasted_iota(jnp.int32, (wide, wide), 1) % GROUP
    )
    kron[...] = jnp.where(same, spread_out, 0.0).astype(jnp.bfloat16)


def mix(env_refs, offset, mps_ref, spread, bond, flat, deep, flat_at, deep_at):
    block = mps_ref.shape[-1]
    first_block = 0 if offset == 0 else len(MPS_BLOCKS) // 2
    level, falling = mps_ref[first_block], mps_ref[first_block + 2]
    right = jnp.concatenate([level, falling], axis=1)
    per_chunk = bond // len(env_refs)
    for index, ref in enumerate(env_refs):
        if len(env_refs) == 1:
            first, rows = 0, (ref[:, 0], ref[:, 1])
        else:
            op_pos = lax.axis_index("op")
            first = jnp.bitwise_xor(op_pos, index) * per_chunk
            at = lax.rem(op_pos, spread) + 1 + offset
            rows = (ref[:, at, 0], ref[:, at, 1])
        low, high = (
            jnp.dot(
                part.reshape(per_chunk * block, block), other, preferred_element_type=jnp.float32
            )
            for part, other in zip(rows, (right, mps_ref[first_block + 1]))
        )
        shape = (per_chunk, block, block)
        flat[pl.ds(flat_at + first, per_chunk)] = low[:, :block].reshape(shape)
        deep[pl.ds(deep_at + bond + first, per_chunk)] = low[:, block:].reshape(shape)
        deep[pl.ds(deep_at + first, per_chunk)] = high.reshape(shape)


def contract(mixed, left, store):
    block = mixed.shape[-1]
    rows, columns = left.shape
    used = columns // GROUP

    def body(index, carry):
        at = pl.multiple_of(index * 2 * GROUP, 2 * GROUP)
        low = mixed[:used, pl.ds(at, GROUP), :].reshape(columns, block)
        high = mixed[:used, pl.ds(at + GROUP, GROUP), :].reshape(columns, block)
        right = jnp.concatenate([low, high], axis=1).astype(jnp.bfloat16)
        got = jnp.dot(left, right, preferred_element_type=jnp.float32)
        store(
            at,
            got[:, :block].reshape(rows // GROUP, GROUP, block),
            got[:, block:].reshape(rows // GROUP, GROUP, block),
        )
        return carry

    steps = block // (2 * GROUP)
    lax.fori_loop(0, steps, body, 0, unroll=steps)


def left_rows(pairs, kept_rows, spread):
    if kept_rows == pairs:
        return pl.ds(0, pairs * GROUP)
    layer = lax.axis_index("op") // spread
    return pl.ds(pl.multiple_of(layer * (kept_rows * GROUP), kept_rows * GROUP), kept_rows * GROUP)


def own_kernel(spread, bond, mps_ref, kron, env_ref, out_ref, flat, deep):
    mix([env_ref], 0, mps_ref, spread, bond, flat, deep, 0, 0)
    for down, (mixed, states) in enumerate(((flat, 1), (deep, 2))):

        def store(at, low, high):
            out_ref[down, :, pl.ds(at, GROUP), :] = low
            out_ref[down, :, pl.ds(at + GROUP, GROUP), :] = high

        contract(mixed, kron[:, : states * bond * GROUP], store)


def project(down, row, kept_bonds, first_bond, charges, turned, summed, write):
    block = summed.shape[-1]
    for index in range(kept_bonds):
        bond_index = first_bond + index
        up = charges[bond_index, 0]
        target = down + charges[bond_index, 1]
        inside = (row + up >= 0) & (row + up < UP_VALUES) & (target >= 0) & (target < DOWN_VALUES)
        entry = jnp.where(inside, (up + 1) * DOWN_VALUES + target, ROW_SHIFTS * DOWN_VALUES)
        right = (
            summed[index * PHYS : (index + 1) * PHYS]
            .reshape(PHYS * block, block)
            .astype(jnp.bfloat16)
        )
        value = jnp.dot(turned[entry], right, preferred_element_type=jnp.float32)
        write(index, value)


def keep_part(spread, out_ref, keep_ref):
    count = keep_ref.shape[0]
    keep_ref[...] = out_ref[pl.ds(lax.axis_index("op") // spread * count, count)]


def first_kernel(chain_count, spread, bond, chunks, charges, mps_ref, turned, kron, *refs):
    env_refs, (out_ref, keep_ref, flat, deep, summed) = refs[:chunks], refs[chunks:]
    row = my_row(chain_count, spread)
    mix(env_refs, 0, mps_ref, spread, bond, flat, deep, 0, 0)
    mix(env_refs, -1, mps_ref, spread, bond, flat, deep, bond, 2 * bond)
    step = bond * GROUP
    level = jnp.concatenate([kron[:, :step], kron[:, 2 * step : 3 * step]], axis=1)
    for down, (mixed, left) in enumerate(((flat, level), (deep, kron[...]))):

        def store(at, low, high):
            summed[:, pl.ds(at, GROUP), :] = low
            summed[:, pl.ds(at + GROUP, GROUP), :] = high

        def write(index, value):
            out_ref[index, down] = value.astype(jnp.bfloat16)

        contract(mixed, left, store)
        project(down, row, bond, 0, charges, turned, summed, write)
    keep_part(spread, out_ref, keep_ref)


def main_kernel(
    chain_count, spread, bond, outer, charges, mps_ref, turned, kron, own_ref, env_ref, *refs
):
    inner_ref, refs = (refs[0], refs[1:]) if outer and spread > 1 else (None, refs)
    out_ref, refs = refs[0], refs[1:]
    keep_ref, refs = (refs[0], refs[1:]) if outer else (None, refs)
    flat, deep, summed = refs
    row = my_row(chain_count, spread)
    half = 2 * bond * GROUP
    from_outside = lax.rem(lax.axis_index("op"), spread) == 0

    def compute():
        mix([env_ref], -1, mps_ref, spread, bond, flat, deep, 0, 0)
        for down, (mixed, states) in enumerate(((flat, 1), (deep, 2))):

            def store(at, low, high):
                summed[:, pl.ds(at, GROUP), :] = low + own_ref[down, :, pl.ds(at, GROUP), :]
                summed[:, pl.ds(at + GROUP, GROUP), :] = (
                    high + own_ref[down, :, pl.ds(at + GROUP, GROUP), :]
                )

            def write(index, value):
                out_ref[index, down] = value.astype(jnp.bfloat16)

            contract(mixed, kron[:, half : half + states * bond * GROUP], store)
            project(down, row, bond, 0, charges, turned, summed, write)

    pl.when(from_outside if outer else jnp.logical_not(from_outside))(compute)
    if inner_ref is not None:

        @pl.when(jnp.logical_not(from_outside))
        def _():
            out_ref[...] = inner_ref[...]

    if outer:
        keep_part(spread, out_ref, keep_ref)


def part_kernel(
    chain_count, spread, bond, ahead, charges, mps_ref, turned, kron, env_ref, out_ref,
    flat, deep, summed
):
    row = my_row(chain_count, spread) + ahead
    kept_bonds = out_ref.shape[0]
    rows = left_rows(bond * PHYS, kept_bonds * PHYS, spread)
    start = ahead * 2 * bond * GROUP
    first_bond = lax.axis_index("op") // spread * kept_bonds
    mix([env_ref], -ahead, mps_ref, spread, bond, flat, deep, 0, 0)
    for down, (mixed, states) in enumerate(((flat, 1), (deep, 2))):

        def store(at, low, high):
            summed[:, pl.ds(at, GROUP), :] = low
            summed[:, pl.ds(at + GROUP, GROUP), :] = high

        def write(index, value):
            out_ref[index, down] = value.astype(out_ref.dtype)

        contract(mixed, kron[rows, start : start + states * bond * GROUP], store)
        project(down, row, kept_bonds, first_bond, charges, turned, summed, write)


def sort_kernel(chain_count, spread, own_ref, before_ref, *refs):
    kept_refs, refs = refs[: chain_count - 1], refs[chain_count - 1 :]
    out_refs, result = refs[:-1], refs[-1]
    result[...] = (own_ref[...] + before_ref[...].astype(jnp.float32)).astype(jnp.bfloat16)
    chain_pos = lax.axis_index("chain")
    side = lax.rem(lax.axis_index("op"), spread)
    count = result.shape[0] // spread
    sources = list(kept_refs) + [result]
    for hop in range(chain_count):
        target_chain = jnp.bitwise_xor(chain_pos, hop)
        for turn in range(spread):
            first = jnp.bitwise_xor(side, turn) * count
            for source_site, source in enumerate(sources):
                @pl.when(target_chain == source_site)
                def _():
                    out_refs[hop * spread + turn][...] = source[pl.ds(first, count)]


def gather_kernel(chain_count, spread, *refs):
    out_ref = refs[-1]
    chain_pos = lax.axis_index("chain")
    side = lax.rem(lax.axis_index("op"), spread)
    for hop in range(chain_count):
        for turn in range(spread):
            row = place(jnp.bitwise_xor(chain_pos, hop), chain_count) * spread
            row = row + jnp.bitwise_xor(side, turn)
            out_ref[0, :, pl.ds(row * DOWN_VALUES, DOWN_VALUES)] = refs[hop * spread + turn][...]


def sweep(env_in, mps, proj, mpo, mpo_charge, block_sizes):
    chain_count = lax.axis_size("chain")
    op_count = lax.axis_size("op")
    local_bond, sectors, block, _ = env_in.shape
    bond = mpo_charge.shape[0]
    pairs = bond * PHYS
    sites = block_sizes.shape[0] - 1
    spread = UP_VALUES // chain_count
    both = ("chain", "op")
    everyone = [(c, o) for c in range(chain_count) for o in range(op_count)]
    square = (block, block)

    def flat(chain, op):
        return chain * op_count + op

    packed = call(
        functools.partial(pack_env_kernel, chain_count, spread),
        shape_of(local_bond, spread + 1, DOWN_VALUES, *square),
        [HBM],
        [env_in.reshape(local_bond, UP_VALUES, DOWN_VALUES, *square)],
        [pltpu.SemaphoreType.DMA((2 * local_bond,))],
        limit=60,
        place_out=VMEM,
    )
    own_packed = call(
        functools.partial(pack_env_kernel, chain_count, spread),
        shape_of(local_bond, spread + 1, DOWN_VALUES, *square),
        [ANY],
        [env_in.reshape(local_bond, UP_VALUES, DOWN_VALUES, *square)],
        [pltpu.SemaphoreType.DMA((2 * local_bond,))],
    )
    received = [packed]
    for hop in range(spread, op_count, spread):
        received.append(lax.ppermute(packed, "op", [(o, o ^ hop) for o in range(op_count)]))
    chunks = []
    for piece in received:
        chunks.append(piece)
        for turn in range(1, spread):
            chunks.append(lax.ppermute(piece, "op", [(o, o ^ turn) for o in range(op_count)]))
    chunks[0] = own_packed

    blocks = proj_start(None, spread)
    far = chain_count - 1
    moves = len(MPS_PARTS) + sum(part[2] for part in PROJ_PARTS)
    tensors = [mps, proj.reshape(1, PHYS, UP_VALUES, DOWN_VALUES, *square)]
    parcels = call(
        functools.partial(pack_site_kernel, chain_count, spread, 1),
        [shape_of(blocks, *square)] * far,
        [HBM, HBM],
        tensors,
        [pltpu.SemaphoreType.DMA((moves * far,))],
        limit=60,
        place_out=VMEM,
    )
    parcels = call(
        functools.partial(pack_site_kernel, chain_count, spread, 0),
        [shape_of(blocks, *square)],
        [ANY, ANY],
        tensors,
        [pltpu.SemaphoreType.DMA((moves,))],
    ) + parcels
    weights = [parcels[0]]
    for hop in range(1, far):
        weights.append(
            lax.ppermute(parcels[hop], "chain", [(c, c ^ hop) for c in range(chain_count)])
        )
    weights.append(lax.ppermute(parcels[far], "chain", [(0, far)]))
    weights.append(
        lax.ppermute(parcels[far], "chain", [(c, c ^ far) for c in range(1, chain_count)])
    )
    turned_weights = []
    for piece in weights:
        turned_weights.append(
            [piece]
            + [
                lax.ppermute(piece, "op", [(o, o ^ turn) for o in range(op_count)])
                for turn in range(1, spread)
            ]
        )
    weights = turned_weights
    matrix = mpo_matrix(mpo[0])
    matrix = jnp.pad(matrix, ((0, 0), (0, block - matrix.shape[1])))
    matrices = [matrix]
    for hop in range(1, chain_count):
        matrices.append(lax.ppermute(matrix, "chain", [(c, c ^ hop) for c in range(chain_count)]))
    mask = call(mask_kernel, shape_of(pairs, block, dtype=jnp.float32), [SMEM], [mpo_charge])

    inner_halo, outer_halo = [], []
    for c, o in everyone:
        at = place(c, chain_count)
        if o % spread < spread - 1:
            inner_halo.append((flat(c, o), flat(c, o + 1)))
        elif at < chain_count - 1:
            outer_halo.append(
                (flat(c, o), flat(ring_chain(at + 1, chain_count), o - spread + 1))
            )
    halo = inner_halo + outer_halo

    keep = local_bond * spread
    kept = []
    turn = (spread - 1) ^ ((ROW_SHIFTS - 1) // held_rows(spread))
    late = weights[:far] + [weights[far + 1]]
    extra_count = sum(part[2] for part in PROJ_PARTS)
    extra = call(
        functools.partial(pick_extra_kernel, sites - 1, chain_count, spread),
        shape_of(extra_count, *square),
        [ANY] * chain_count,
        [pieces[turn] for pieces in late],
        [pltpu.SemaphoreType.DMA((extra_count,))],
    )
    extra = lax.ppermute(
        extra,
        both,
        [
            (flat(ring_chain(at + 1, chain_count), o), flat(ring_chain(at, chain_count), o))
            for at in range(chain_count - 1)
            for o in range(spread - 1, op_count, spread)
        ],
    )
    mixed_scratch = [
        pltpu.VMEM((bond, *square), jnp.float32),
        pltpu.VMEM((2 * bond, *square), jnp.float32),
    ]
    table = shape_of(ROW_SHIFTS * DOWN_VALUES + 1, block, PHYS * block)
    full = [shape_of(bond, DOWN_VALUES, *square), shape_of(keep, DOWN_VALUES, *square)]
    for site in range(sites):
        last = site == sites - 1
        masked, turned, kron, *more = call(
            functools.partial(
                prep_kernel, site, last, chain_count, spread, bond, block, chain_count
            ),
            [
                shape_of(len(MPS_BLOCKS), *square),
                table,
                shape_of(pairs * GROUP, pairs * GROUP),
            ]
            + [table] * last,
            [SMEM, VMEM]
            + [VMEM] * chain_count
            + [ANY] * (chain_count * spread)
            + [VMEM] * last,
            [block_sizes, mask]
            + matrices
            + sum(weights[:far], [])
            + weights[far + 1 if site else far]
            + [extra] * last,
            [
                pltpu.VMEM((spread, blocks, *square), jnp.bfloat16),
                pltpu.SemaphoreType.DMA((spread,)),
            ],
        )
        if site == 0:
            finished, part = call(
                functools.partial(first_kernel, chain_count, spread, bond, len(chunks)),
                full,
                [SMEM] + [VMEM] * (3 + len(chunks)),
                [mpo_charge, masked, turned, kron] + chunks,
                [
                    pltpu.VMEM((2 * bond, *square), jnp.float32),
                    pltpu.VMEM((4 * bond, *square), jnp.float32),
                    pltpu.VMEM((pairs, *square), jnp.float32),
                ],
                limit=28,
            )
            kept.append(part)
            leaving = finished
        elif not last:
            own = call(
                functools.partial(own_kernel, spread, bond),
                shape_of(DOWN_VALUES, pairs, *square, dtype=jnp.float32),
                [VMEM] * 3,
                [masked, kron, finished],
                mixed_scratch,
            )
            shared = [mpo_charge, masked, turned, kron, own]
            scratch = mixed_scratch + [pltpu.VMEM((pairs, *square), jnp.float32)]
            outside = lax.ppermute(leaving, both, outer_halo)
            passed = []
            if spread > 1:
                inside = lax.ppermute(finished, both, inner_halo)
                passed.append(
                    call(
                        functools.partial(main_kernel, chain_count, spread, bond, False),
                        full[0],
                        [SMEM] + [VMEM] * 5,
                        shared + [inside],
                        scratch,
                        limit=28,
                    )
                )
            finished, part = call(
                functools.partial(main_kernel, chain_count, spread, bond, True),
                full,
                [SMEM] + [VMEM] * (5 + len(passed)),
                shared + [outside] + passed,
                scratch,
                limit=28,
            )
            leaving = passed[0] if spread == 2 else finished
            kept.append(part)
        else:
            parts = [
                call(
                    functools.partial(part_kernel, chain_count, spread, bond, ahead),
                    shape_of(keep, DOWN_VALUES, *square, dtype=dtype),
                    [SMEM] + [VMEM] * 4,
                    [mpo_charge, masked, entries, kron, finished],
                    mixed_scratch + [pltpu.VMEM((keep * PHYS, *square), jnp.float32)],
                    limit=28,
                )
                for ahead, entries, dtype in (
                    (1, more[0], jnp.bfloat16),
                    (0, turned, jnp.float32),
                )
            ]
            before = lax.ppermute(parts[0], both, halo)
            results = call(
                functools.partial(sort_kernel, chain_count, spread),
                [shape_of(local_bond, DOWN_VALUES, *square)] * (chain_count * spread),
                [VMEM] * (2 + len(kept)),
                [parts[1], before] + kept,
                [pltpu.VMEM((keep, DOWN_VALUES, *square), jnp.bfloat16)],
            )

    arrived = []
    for hop in range(chain_count):
        for turn in range(spread):
            piece = results[hop * spread + turn]
            if hop or turn:
                piece = lax.ppermute(
                    piece, both, [(flat(c, o), flat(c ^ hop, o ^ turn)) for c, o in everyone]
                )
            arrived.append(piece)
    return call(
        functools.partial(gather_kernel, chain_count, spread),
        shape_of(1, local_bond, sectors, *square),
        [VMEM] * len(arrived),
        arrived,
    )


def solution(mesh):
    return jax.shard_map(
        sweep,
        mesh=mesh,
        in_specs=(
            P("op", None, None, None),
            P("chain", None, None, None, None),
            P("chain", None, None, None, None),
            P("chain", None, None, None, None),
            P(),
            P(),
        ),
        out_specs=P("chain", "op", None, None, None),
        check_vma=False,
    )
```

profile of v0, /device:TPU:27, one launch (start us, length us, event | category | flops | bytes accessed | tf_op | source)
XLA Modules:
  0.0 160.9 jit_solution(16268796564397153450)
XLA Ops:
  0.0 3.0 %shard_map.66 = (bf16[18,128,128]{2,1,0:T(8,128)(2,1)}, bf16[18,128,128]{2,1,0:T(8,128)(2,1)}, bf16[18,128,128]{2,1,0:T(8,128)(2,1)}) custom-call(bf16[1,4,16,128,128]{4,3,2,1,0:T(8,128)(2,1)} %mps_ref.3, bf16[1,4,8,2,128,128]{5,4,3,2,1,0:T(8,128)(2,1)} %bitcast.5), custom_call_target="tpu_custom_call" | custom-call | flops 100000000 | bytes 1000000 | tf_op jit(solution)/shard_map/pallas_call | solution.py:77
  4.5 1.8 %shard_map.73 = bf16[2,3,2,128,128]{4,3,2,1,0:T(8,128)(2,1)} custom-call(bf16[2,8,2,128,128]{4,3,2,1,0:T(8,128)(2,1)} %bitcast.7), custom_call_target="tpu_custom_call" | custom-call | flops 100000000 | bytes 1000000 | tf_op jit(solution)/shard_map/pallas_call | solution.py:77
  6.5 1.5 collective-permute-start.11
  10.3 8.6 %collective-permute-done.2.refs_3_ = bf16[64,128]{1,0:T(8,128)(2,1)S(1)} collective-permute-done((bf16[64,128]{1,0:T(8,128)(2,1)S(1)}, bf16[64,128]{1,0:T(8,128)(2,1)S(1)}, u32[]{:S(2)}, u32[]{:S(2)}) %collective-permute-start.2) | collective-permute-done | bytes 16416 | tf_op jit(solution)/shard_map/ppermute | solution.py:568
  19.5 12.9 %collective-permute-start.1 = (bf16[64,128]{1,0:T(8,128)(2,1)S(1)}, bf16[64,128]{1,0:T(8,128)(2,1)S(1)}, u32[]{:S(2)}, u32[]{:S(2)}) collective-permute-start(bf16[64,128]{1,0:T(8,128)(2,1)S(1)} %pad.4.refs_0_), channel_id=1, source_target_pairs={{0,16},{8,24},{16,0},{24,8},{1,17},{9,25},{17,1},{25,9},{2,18},{10... | collective-permute-start | bytes 49160 | tf_op jit(solution)/shard_map/ppermute | solution.py:568
  34.7 2.0 %collective-permute-done.refs_1_ = bf16[64,128]{1,0:T(8,128)(2,1)S(1)} collective-permute-done((bf16[64,128]{1,0:T(8,128)(2,1)S(1)}, bf16[64,128]{1,0:T(8,128)(2,1)S(1)}, u32[]{:S(2)}, u32[]{:S(2)}) %collective-permute-start) | collective-permute-done | bytes 16416 | tf_op jit(solution)/shard_map/ppermute | solution.py:568
  37.4 1.6 copy-done.3
  38.9 1.6 copy-done.4
  41.1 3.8 %collective-permute-start.3 = (bf16[18,128,128]{2,1,0:T(8,128)(2,1)S(1)}, bf16[18,128,128]{2,1,0:T(8,128)(2,1)S(1)}, u32[]{:S(2)}, u32[]{:S(2)}) collective-permute-start(bf16[18,128,128]{2,1,0:T(8,128)(2,1)S(1)} %shard_map.65.refs_0_.refs_4_), channel_id=1, source_target_pairs={{0,1},{1,0},{2,3},{3,2},{4,5},{5,4},{6,7},{7,6},{8,9},{9,8},{10,11... | collective-permute-start | bytes 1769480 | tf_op jit(solution)/shard_map/ppermute | solution.py:559
  45.5 12.4 %collective-permute-done.16.refs_4_ = bf16[2,3,2,128,128]{4,3,2,1,0:T(8,128)(2,1)} collective-permute-done((bf16[2,3,2,128,128]{4,3,2,1,0:T(8,128)(2,1)}, bf16[2,3,2,128,128]{4,3,2,1,0:T(8,128)(2,1)}, u32[]{:S(2)}, u32[]{:S(2)}) %collective-permute-start.16) | collective-permute-done | bytes 393248 | tf_op jit(solution)/shard_map/ppermute | solution.py:517
  58.4 10.0 %collective-permute-done.14.refs_2_ = bf16[2,3,2,128,128]{4,3,2,1,0:T(8,128)(2,1)} collective-permute-done((bf16[2,3,2,128,128]{4,3,2,1,0:T(8,128)(2,1)}, bf16[2,3,2,128,128]{4,3,2,1,0:T(8,128)(2,1)}, u32[]{:S(2)}, u32[]{:S(2)}) %collective-permute-start.14) | collective-permute-done | bytes 393248 | tf_op jit(solution)/shard_map/ppermute | solution.py:517
  71.9 3.1 %collective-permute-start.8 = (bf16[18,128,128]{2,1,0:T(8,128)(2,1)}, bf16[18,128,128]{2,1,0:T(8,128)(2,1)S(1)}, u32[]{:S(2)}, u32[]{:S(2)}) collective-permute-start(bf16[18,128,128]{2,1,0:T(8,128)(2,1)} %get-tuple-element.37), channel_id=1, source_target_pairs={{8,16},{16,8},{24,0},{9,17},{17,9},{25,1},{10,18},{18,10},{26,2},{... | collective-permute-start | bytes 1769480 | tf_op jit(solution)/shard_map/ppermute | solution.py:552
  84.1 5.8 %shard_map.74 = (bf16[16,2,128,128]{3,2,1,0:T(8,128)(2,1)S(1)}, bf16[4,2,128,128]{3,2,1,0:T(8,128)(2,1)S(1)}) custom-call(s32[16,2]{1,0:T(8,128)S(1)} %copy.14.charges, bf16[6,128,128]{2,1,0:T(8,128)(2,1)S(1)} %get-tuple-element.47.mps_ref, bf16[7,128,512]{2,1,0:T(8,128)(2,1)S(1)} %get-tuple-element.48.turned, bf16[512,512]{1,0:T(8,128)(2,1)S(1)} %get-tuple-element.49.kron, ...), custom_call_target="tpu_custom_call" | custom-call | flops 100000000 | bytes 1000000 | tf_op jit(solution)/shard_map/pallas_call | solution.py:77
  91.2 3.9 %collective-permute-start.20 = (bf16[16,2,128,128]{3,2,1,0:T(8,128)(2,1)S(1)}, bf16[16,2,128,128]{3,2,1,0:T(8,128)(2,1)S(1)}, u32[]{:S(2)}, u32[]{:S(2)}) collective-permute-start(bf16[16,2,128,128]{3,2,1,0:T(8,128)(2,1)S(1)} %get-tuple-element.50.env_ref), channel_id=1, source_target_pairs={{1,8},{3,10},{5,12},{7,14},{9,24},{11,26},{13,28},{15,30},{17,0},{... | collective-permute-start | bytes 3145736 | tf_op jit(solution)/shard_map/ppermute | solution.py:660
  95.2 2.0 %collective-permute-done.9.refs_11_ = bf16[18,128,128]{2,1,0:T(8,128)(2,1)S(1)} collective-permute-done((bf16[18,128,128]{2,1,0:T(8,128)(2,1)S(1)}, bf16[18,128,128]{2,1,0:T(8,128)(2,1)S(1)}, u32[]{:S(2)}, u32[]{:S(2)}) %collective-permute-start.9) | collective-permute-done | bytes 589856 | tf_op jit(solution)/shard_map/ppermute | solution.py:559
  98.6 2.0 %shard_map.75.own_ref = f32[2,64,128,128]{3,2,1,0:T(8,128)S(1)} custom-call(bf16[6,128,128]{2,1,0:T(8,128)(2,1)S(1)} %get-tuple-element.44.mps_ref, bf16[512,512]{1,0:T(8,128)(2,1)S(1)} %get-tuple-element.46.kron, bf16[16,2,128,128]{3,2,1,0:T(8,128)(2,1)S(1)} %get-tuple-element.50.env_ref), custom_call_target="tpu_custom_call" | custom-call | flops 100000000 | bytes 1000000 | tf_op jit(solution)/shard_map/pallas_call | solution.py:77
  100.7 4.2 %shard_map.76.refs_0_ = bf16[16,2,128,128]{3,2,1,0:T(8,128)(2,1)S(1)} custom-call(s32[16,2]{1,0:T(8,128)S(1)} %copy.14.charges, bf16[6,128,128]{2,1,0:T(8,128)(2,1)S(1)} %get-tuple-element.44.mps_ref, bf16[7,128,512]{2,1,0:T(8,128)(2,1)S(1)} %get-tuple-element.45.turned, bf16[512,512]{1,0:T(8,128)(2,1)S(1)} %get-tuple-element.46.kron, ...), custom_call_target="tpu_custom_call" | custom-call | flops 100000000 | bytes 1000000 | tf_op jit(solution)/shard_map/pallas_call | solution.py:77
  104.9 1.9 %collective-permute-done.20.env_ref = bf16[16,2,128,128]{3,2,1,0:T(8,128)(2,1)S(1)} collective-permute-done((bf16[16,2,128,128]{3,2,1,0:T(8,128)(2,1)S(1)}, bf16[16,2,128,128]{3,2,1,0:T(8,128)(2,1)S(1)}, u32[]{:S(2)}, u32[]{:S(2)}) %collective-permute-start.20) | collective-permute-done | bytes 1048608 | tf_op jit(solution)/shard_map/ppermute | solution.py:660
  108.9 7.8 %collective-permute-start.22 = (bf16[16,2,128,128]{3,2,1,0:T(8,128)(2,1)S(1)}, bf16[16,2,128,128]{3,2,1,0:T(8,128)(2,1)S(1)}, u32[]{:S(2)}, u32[]{:S(2)}) collective-permute-start(bf16[16,2,128,128]{3,2,1,0:T(8,128)(2,1)S(1)} %shard_map.76.refs_0_), channel_id=1, source_target_pairs={{1,8},{3,10},{5,12},{7,14},{9,24},{11,26},{13,28},{15,30},{17,0},{... | collective-permute-start | bytes 3145736 | tf_op jit(solution)/shard_map/ppermute | solution.py:660
  117.1 2.5 %collective-permute-start.10 = (bf16[6,128,128]{2,1,0:T(8,128)(2,1)S(1)}, bf16[6,128,128]{2,1,0:T(8,128)(2,1)S(1)}, u32[]{:S(2)}, u32[]{:S(2)}) collective-permute-start(bf16[6,128,128]{2,1,0:T(8,128)(2,1)S(1)} %shard_map.67), channel_id=1, source_target_pairs={{1,17},{3,19},{5,21},{7,23},{9,1},{11,3},{13,5},{15,7},{25,9},{27,... | collective-permute-start | bytes 589832 | tf_op jit(solution)/shard_map/ppermute | solution.py:594
  121.0 2.8 %collective-permute-done.10.refs_12_ = bf16[6,128,128]{2,1,0:T(8,128)(2,1)S(1)} collective-permute-done((bf16[6,128,128]{2,1,0:T(8,128)(2,1)S(1)}, bf16[6,128,128]{2,1,0:T(8,128)(2,1)S(1)}, u32[]{:S(2)}, u32[]{:S(2)}) %collective-permute-start.10) | collective-permute-done | bytes 196640 | tf_op jit(solution)/shard_map/ppermute | solution.py:594
  123.8 1.5 shard_map.68
  125.2 2.0 %shard_map.78.own_ref = f32[2,64,128,128]{3,2,1,0:T(8,128)S(1)} custom-call(bf16[6,128,128]{2,1,0:T(8,128)(2,1)S(1)} %get-tuple-element.41.mps_ref, bf16[512,512]{1,0:T(8,128)(2,1)S(1)} %get-tuple-element.43.kron, bf16[16,2,128,128]{3,2,1,0:T(8,128)(2,1)S(1)} %get-tuple-element.51.env_ref), custom_call_target="tpu_custom_call" | custom-call | flops 100000000 | bytes 1000000 | tf_op jit(solution)/shard_map/pallas_call | solution.py:77
  127.3 4.2 %shard_map.79.refs_0_ = bf16[16,2,128,128]{3,2,1,0:T(8,128)(2,1)S(1)} custom-call(s32[16,2]{1,0:T(8,128)S(1)} %copy.14.charges, bf16[6,128,128]{2,1,0:T(8,128)(2,1)S(1)} %get-tuple-element.41.mps_ref, bf16[7,128,512]{2,1,0:T(8,128)(2,1)S(1)} %get-tuple-element.42.turned, bf16[512,512]{1,0:T(8,128)(2,1)S(1)} %get-tuple-element.43.kron, ...), custom_call_target="tpu_custom_call" | custom-call | flops 100000000 | bytes 1000000 | tf_op jit(solution)/shard_map/pallas_call | solution.py:77
  132.3 2.4 %shard_map.82 = bf16[4,2,128,128]{3,2,1,0:T(8,128)(2,1)S(1)} custom-call(s32[16,2]{1,0:T(8,128)S(1)} %copy.14.charges, bf16[6,128,128]{2,1,0:T(8,128)(2,1)S(1)} %get-tuple-element.38.mps_ref, bf16[7,128,512]{2,1,0:T(8,128)(2,1)S(1)} %get-tuple-element.53.turned, bf16[512,512]{1,0:T(8,128)(2,1)S(1)} %get-tuple-element.40.kron, ...), custom_call_target="tpu_custom_call" | custom-call | flops 100000000 | bytes 1000000 | tf_op jit(solution)/shard_map/pallas_call | solution.py:77
  134.7 4.5 %collective-permute-start.24 = (bf16[4,2,128,128]{3,2,1,0:T(8,128)(2,1)S(1)}, bf16[4,2,128,128]{3,2,1,0:T(8,128)(2,1)S(1)}, u32[]{:S(2)}, u32[]{:S(2)}) collective-permute-start(bf16[4,2,128,128]{3,2,1,0:T(8,128)(2,1)S(1)} %shard_map.82), channel_id=1, source_target_pairs={{0,1},{2,3},{4,5},{6,7},{8,9},{10,11},{12,13},{14,15},{16,17},{18,... | collective-permute-start | bytes 786440 | tf_op jit(solution)/shard_map/ppermute | solution.py:699
  139.2 2.4 %shard_map.81.own_ref = f32[4,2,128,128]{3,2,1,0:T(8,128)S(1)} custom-call(s32[16,2]{1,0:T(8,128)S(1)} %copy.14.charges, bf16[6,128,128]{2,1,0:T(8,128)(2,1)S(1)} %get-tuple-element.38.mps_ref, bf16[7,128,512]{2,1,0:T(8,128)(2,1)S(1)} %get-tuple-element.39.turned, bf16[512,512]{1,0:T(8,128)(2,1)S(1)} %get-tuple-element.40.kron, ...), custom_call_target="tpu_custom_call" | custom-call | flops 100000000 | bytes 1000000 | tf_op jit(solution)/shard_map/pallas_call | solution.py:77
  142.7 1.8 %collective-permute-start.25 = (bf16[2,2,128,128]{3,2,1,0:T(8,128)(2,1)S(1)}, bf16[2,2,128,128]{3,2,1,0:T(8,128)(2,1)S(1)}, u32[]{:S(2)}, u32[]{:S(2)}) collective-permute-start(bf16[2,2,128,128]{3,2,1,0:T(8,128)(2,1)S(1)} %get-tuple-element.58), channel_id=1, source_target_pairs={{0,1},{1,0},{2,3},{3,2},{4,5},{5,4},{6,7},{7,6},{8,9},{9,8},{10,11... | collective-permute-start | bytes 393224 | tf_op jit(solution)/shard_map/ppermute | solution.py:713
  144.5 1.7 %collective-permute-start.27 = (bf16[2,2,128,128]{3,2,1,0:T(8,128)(2,1)S(1)}, bf16[2,2,128,128]{3,2,1,0:T(8,128)(2,1)S(1)}, u32[]{:S(2)}, u32[]{:S(2)}) collective-permute-start(bf16[2,2,128,128]{3,2,1,0:T(8,128)(2,1)S(1)} %get-tuple-element.60), channel_id=1, source_target_pairs={{0,9},{1,8},{2,11},{3,10},{4,13},{5,12},{6,15},{7,14},{8,1},{9,0},... | collective-permute-start | bytes 393224 | tf_op jit(solution)/shard_map/ppermute | solution.py:713
  149.5 1.7 %collective-permute-start.31 = (bf16[2,2,128,128]{3,2,1,0:T(8,128)(2,1)S(1)}, bf16[2,2,128,128]{3,2,1,0:T(8,128)(2,1)S(1)}, u32[]{:S(2)}, u32[]{:S(2)}) collective-permute-start(bf16[2,2,128,128]{3,2,1,0:T(8,128)(2,1)S(1)} %get-tuple-element.64), channel_id=1, source_target_pairs={{0,25},{1,24},{2,27},{3,26},{4,29},{5,28},{6,31},{7,30},{8,17},{9,... | collective-permute-start | bytes 393224 | tf_op jit(solution)/shard_map/ppermute | solution.py:713
  151.1 2.2 %collective-permute-done.27.refs_3_ = bf16[2,2,128,128]{3,2,1,0:T(8,128)(2,1)S(1)} collective-permute-done((bf16[2,2,128,128]{3,2,1,0:T(8,128)(2,1)S(1)}, bf16[2,2,128,128]{3,2,1,0:T(8,128)(2,1)S(1)}, u32[]{:S(2)}, u32[]{:S(2)}) %collective-permute-start.27) | collective-permute-done | bytes 131104 | tf_op jit(solution)/shard_map/ppermute | solution.py:713
  153.4 6.5 %collective-permute-done.29.refs_5_ = bf16[2,2,128,128]{3,2,1,0:T(8,128)(2,1)S(1)} collective-permute-done((bf16[2,2,128,128]{3,2,1,0:T(8,128)(2,1)S(1)}, bf16[2,2,128,128]{3,2,1,0:T(8,128)(2,1)S(1)}, u32[]{:S(2)}, u32[]{:S(2)}) %collective-permute-start.29) | collective-permute-done | bytes 131104 | tf_op jit(solution)/shard_map/ppermute | solution.py:713
  (103 shorter events, 34.5 us)
Async XLA Ops:
  3.0 42.0 %collective-permute-start.4 = (bf16[18,128,128]{2,1,0:T(8,128)(2,1)}, bf16[18,128,128]{2,1,0:T(8,128)(2,1)S(1)}, u32[]{:S(2)}, u32[]{:S(2)}) collective-permute-start(bf16[18,128,128]{2,1,0:T(8,128)(2,1)} %get-tuple-element.35), channel_id=1, source_target_pairs={{0,8},{8,0},{16,24},{24,16},{1,9},{9,1},{17,25},{25,17},{2,10},{10... | collective-permute-start | bytes 1769480 | tf_op jit(solution)/shard_map/ppermute | solution.py:548
  3.3 41.8 %collective-permute-start.6 = (bf16[18,128,128]{2,1,0:T(8,128)(2,1)}, bf16[18,128,128]{2,1,0:T(8,128)(2,1)S(1)}, u32[]{:S(2)}, u32[]{:S(2)}) collective-permute-start(bf16[18,128,128]{2,1,0:T(8,128)(2,1)} %get-tuple-element.36), channel_id=1, source_target_pairs={{0,16},{8,24},{16,0},{24,8},{1,17},{9,25},{17,1},{25,9},{2,18},{10... | collective-permute-start | bytes 1769480 | tf_op jit(solution)/shard_map/ppermute | solution.py:548
  6.4 34.8 %collective-permute-start.18 = (bf16[2,3,2,128,128]{4,3,2,1,0:T(8,128)(2,1)}, bf16[2,3,2,128,128]{4,3,2,1,0:T(8,128)(2,1)}, u32[]{:S(2)}, u32[]{:S(2)}) collective-permute-start(bf16[2,3,2,128,128]{4,3,2,1,0:T(8,128)(2,1)} %shard_map.73), channel_id=1, source_target_pairs={{0,6},{1,7},{2,4},{3,5},{4,2},{5,3},{6,0},{7,1},{8,14},{9,15},{10,... | collective-permute-start | bytes 1179656 | tf_op jit(solution)/shard_map/ppermute | solution.py:517
  6.5 51.4 %collective-permute-start.11 = (bf16[18,128,128]{2,1,0:T(8,128)(2,1)}, bf16[18,128,128]{2,1,0:T(8,128)(2,1)}, u32[]{:S(2)}, u32[]{:S(2)}) collective-permute-start(bf16[18,128,128]{2,1,0:T(8,128)(2,1)} %get-tuple-element.37), channel_id=1, source_target_pairs={{0,24},{1,25},{2,26},{3,27},{4,28},{5,29},{6,30},{7,31}} | collective-permute-start | bytes 1769480 | tf_op jit(solution)/shard_map/ppermute | solution.py:550
  9.1 9.8 %collective-permute-start.2 = (bf16[64,128]{1,0:T(8,128)(2,1)S(1)}, bf16[64,128]{1,0:T(8,128)(2,1)S(1)}, u32[]{:S(2)}, u32[]{:S(2)}) collective-permute-start(bf16[64,128]{1,0:T(8,128)(2,1)S(1)} %pad.4.refs_0_), channel_id=1, source_target_pairs={{0,24},{8,16},{16,8},{24,0},{1,25},{9,17},{17,9},{25,1},{2,26},{10... | collective-permute-start | bytes 49160 | tf_op jit(solution)/shard_map/ppermute | solution.py:568
  19.5 14.0 %collective-permute-start.1 = (bf16[64,128]{1,0:T(8,128)(2,1)S(1)}, bf16[64,128]{1,0:T(8,128)(2,1)S(1)}, u32[]{:S(2)}, u32[]{:S(2)}) collective-permute-start(bf16[64,128]{1,0:T(8,128)(2,1)S(1)} %pad.4.refs_0_), channel_id=1, source_target_pairs={{0,16},{8,24},{16,0},{24,8},{1,17},{9,25},{17,1},{25,9},{2,18},{10... | collective-permute-start | bytes 49160 | tf_op jit(solution)/shard_map/ppermute | solution.py:568
  34.1 2.6 %collective-permute-start = (bf16[64,128]{1,0:T(8,128)(2,1)S(1)}, bf16[64,128]{1,0:T(8,128)(2,1)S(1)}, u32[]{:S(2)}, u32[]{:S(2)}) collective-permute-start(bf16[64,128]{1,0:T(8,128)(2,1)S(1)} %pad.4.refs_0_), channel_id=1, source_target_pairs={{0,8},{8,0},{16,24},{24,16},{1,9},{9,1},{17,25},{25,17},{2,10},{10... | collective-permute-start | bytes 49160 | tf_op jit(solution)/shard_map/ppermute | solution.py:568
  37.3 20.6 %collective-permute-start.16 = (bf16[2,3,2,128,128]{4,3,2,1,0:T(8,128)(2,1)}, bf16[2,3,2,128,128]{4,3,2,1,0:T(8,128)(2,1)}, u32[]{:S(2)}, u32[]{:S(2)}) collective-permute-start(bf16[2,3,2,128,128]{4,3,2,1,0:T(8,128)(2,1)} %shard_map.73), channel_id=1, source_target_pairs={{0,4},{1,5},{2,6},{3,7},{4,0},{5,1},{6,2},{7,3},{8,12},{9,13},{10,... | collective-permute-start | bytes 1179656 | tf_op jit(solution)/shard_map/ppermute | solution.py:517
  41.1 28.6 %collective-permute-start.3 = (bf16[18,128,128]{2,1,0:T(8,128)(2,1)S(1)}, bf16[18,128,128]{2,1,0:T(8,128)(2,1)S(1)}, u32[]{:S(2)}, u32[]{:S(2)}) collective-permute-start(bf16[18,128,128]{2,1,0:T(8,128)(2,1)S(1)} %shard_map.65.refs_0_.refs_4_), channel_id=1, source_target_pairs={{0,1},{1,0},{2,3},{3,2},{4,5},{5,4},{6,7},{7,6},{8,9},{9,8},{10,11... | collective-permute-start | bytes 1769480 | tf_op jit(solution)/shard_map/ppermute | solution.py:559
  45.0 24.7 %collective-permute-start.5 = (bf16[18,128,128]{2,1,0:T(8,128)(2,1)S(1)}, bf16[18,128,128]{2,1,0:T(8,128)(2,1)S(1)}, u32[]{:S(2)}, u32[]{:S(2)}) collective-permute-start(bf16[18,128,128]{2,1,0:T(8,128)(2,1)S(1)} %collective-permute-done.4.refs_1_.refs_6_), channel_id=1, source_target_pairs={{0,1},{1,0},{2,3},{3,2},{4,5},{5,4},{6,7},{7,6},{8,9},{9,8},{10,11... | collective-permute-start | bytes 1769480 | tf_op jit(solution)/shard_map/ppermute | solution.py:559
  45.1 25.2 %collective-permute-start.7 = (bf16[18,128,128]{2,1,0:T(8,128)(2,1)S(1)}, bf16[18,128,128]{2,1,0:T(8,128)(2,1)S(1)}, u32[]{:S(2)}, u32[]{:S(2)}) collective-permute-start(bf16[18,128,128]{2,1,0:T(8,128)(2,1)S(1)} %collective-permute-done.6.refs_2_.refs_8_), channel_id=1, source_target_pairs={{0,1},{1,0},{2,3},{3,2},{4,5},{5,4},{6,7},{7,6},{8,9},{9,8},{10,11... | collective-permute-start | bytes 1769480 | tf_op jit(solution)/shard_map/ppermute | solution.py:559
  57.9 10.5 %collective-permute-start.14 = (bf16[2,3,2,128,128]{4,3,2,1,0:T(8,128)(2,1)}, bf16[2,3,2,128,128]{4,3,2,1,0:T(8,128)(2,1)}, u32[]{:S(2)}, u32[]{:S(2)}) collective-permute-start(bf16[2,3,2,128,128]{4,3,2,1,0:T(8,128)(2,1)} %shard_map.73), channel_id=1, source_target_pairs={{0,2},{1,3},{2,0},{3,1},{4,6},{5,7},{6,4},{7,5},{8,10},{9,11},{10,... | collective-permute-start | bytes 1179656 | tf_op jit(solution)/shard_map/ppermute | solution.py:517
  57.9 13.3 %collective-permute-start.12 = (bf16[18,128,128]{2,1,0:T(8,128)(2,1)}, bf16[18,128,128]{2,1,0:T(8,128)(2,1)S(1)}, u32[]{:S(2)}, u32[]{:S(2)}) collective-permute-start(bf16[18,128,128]{2,1,0:T(8,128)(2,1)} %collective-permute-done.11.refs_10_), channel_id=1, source_target_pairs={{0,1},{1,0},{2,3},{3,2},{4,5},{5,4},{6,7},{7,6},{8,9},{9,8},{10,11... | collective-permute-start | bytes 1769480 | tf_op jit(solution)/shard_map/ppermute | solution.py:559
  68.4 15.7 %collective-permute-start.13 = (bf16[2,3,2,128,128]{4,3,2,1,0:T(8,128)(2,1)}, bf16[2,3,2,128,128]{4,3,2,1,0:T(8,128)(2,1)}, u32[]{:S(2)}, u32[]{:S(2)}) collective-permute-start(bf16[2,3,2,128,128]{4,3,2,1,0:T(8,128)(2,1)} %shard_map.73), channel_id=1, source_target_pairs={{0,1},{1,0},{2,3},{3,2},{4,5},{5,4},{6,7},{7,6},{8,9},{9,8},{10,11... | collective-permute-start | bytes 1179656 | tf_op jit(solution)/shard_map/ppermute | solution.py:522
  69.7 14.4 %collective-permute-start.19 = (bf16[2,3,2,128,128]{4,3,2,1,0:T(8,128)(2,1)}, bf16[2,3,2,128,128]{4,3,2,1,0:T(8,128)(2,1)}, u32[]{:S(2)}, u32[]{:S(2)}) collective-permute-start(bf16[2,3,2,128,128]{4,3,2,1,0:T(8,128)(2,1)} %collective-permute-done.18.refs_6_), channel_id=1, source_target_pairs={{0,1},{1,0},{2,3},{3,2},{4,5},{5,4},{6,7},{7,6},{8,9},{9,8},{10,11... | collective-permute-start | bytes 1179656 | tf_op jit(solution)/shard_map/ppermute | solution.py:522
  69.7 14.4 %collective-permute-start.17 = (bf16[2,3,2,128,128]{4,3,2,1,0:T(8,128)(2,1)}, bf16[2,3,2,128,128]{4,3,2,1,0:T(8,128)(2,1)}, u32[]{:S(2)}, u32[]{:S(2)}) collective-permute-start(bf16[2,3,2,128,128]{4,3,2,1,0:T(8,128)(2,1)} %collective-permute-done.16.refs_4_), channel_id=1, source_target_pairs={{0,1},{1,0},{2,3},{3,2},{4,5},{5,4},{6,7},{7,6},{8,9},{9,8},{10,11... | collective-permute-start | bytes 1179656 | tf_op jit(solution)/shard_map/ppermute | solution.py:522
  71.0 13.0 %collective-permute-start.15 = (bf16[2,3,2,128,128]{4,3,2,1,0:T(8,128)(2,1)}, bf16[2,3,2,128,128]{4,3,2,1,0:T(8,128)(2,1)}, u32[]{:S(2)}, u32[]{:S(2)}) collective-permute-start(bf16[2,3,2,128,128]{4,3,2,1,0:T(8,128)(2,1)} %collective-permute-done.14.refs_2_), channel_id=1, source_target_pairs={{0,1},{1,0},{2,3},{3,2},{4,5},{5,4},{6,7},{7,6},{8,9},{9,8},{10,11... | collective-permute-start | bytes 1179656 | tf_op jit(solution)/shard_map/ppermute | solution.py:522
  71.9 23.2 %collective-permute-start.8 = (bf16[18,128,128]{2,1,0:T(8,128)(2,1)}, bf16[18,128,128]{2,1,0:T(8,128)(2,1)S(1)}, u32[]{:S(2)}, u32[]{:S(2)}) collective-permute-start(bf16[18,128,128]{2,1,0:T(8,128)(2,1)} %get-tuple-element.37), channel_id=1, source_target_pairs={{8,16},{16,8},{24,0},{9,17},{17,9},{25,1},{10,18},{18,10},{26,2},{... | collective-permute-start | bytes 1769480 | tf_op jit(solution)/shard_map/ppermute | solution.py:552
  89.9 10.7 %collective-permute-start.21 = (bf16[16,2,128,128]{3,2,1,0:T(8,128)(2,1)S(1)}, bf16[16,2,128,128]{3,2,1,0:T(8,128)(2,1)S(1)}, u32[]{:S(2)}, u32[]{:S(2)}) collective-permute-start(bf16[16,2,128,128]{3,2,1,0:T(8,128)(2,1)S(1)} %get-tuple-element.50.env_ref), channel_id=1, source_target_pairs={{0,1},{2,3},{4,5},{6,7},{8,9},{10,11},{12,13},{14,15},{16,17},{18,... | collective-permute-start | bytes 3145736 | tf_op jit(solution)/shard_map/ppermute | solution.py:663
  91.2 15.6 %collective-permute-start.20 = (bf16[16,2,128,128]{3,2,1,0:T(8,128)(2,1)S(1)}, bf16[16,2,128,128]{3,2,1,0:T(8,128)(2,1)S(1)}, u32[]{:S(2)}, u32[]{:S(2)}) collective-permute-start(bf16[16,2,128,128]{3,2,1,0:T(8,128)(2,1)S(1)} %get-tuple-element.50.env_ref), channel_id=1, source_target_pairs={{1,8},{3,10},{5,12},{7,14},{9,24},{11,26},{13,28},{15,30},{17,0},{... | collective-permute-start | bytes 3145736 | tf_op jit(solution)/shard_map/ppermute | solution.py:660
  95.2 2.1 %collective-permute-start.9 = (bf16[18,128,128]{2,1,0:T(8,128)(2,1)S(1)}, bf16[18,128,128]{2,1,0:T(8,128)(2,1)S(1)}, u32[]{:S(2)}, u32[]{:S(2)}) collective-permute-start(bf16[18,128,128]{2,1,0:T(8,128)(2,1)S(1)} %collective-permute-done.8.refs_3_.refs_10_), channel_id=1, source_target_pairs={{0,1},{1,0},{2,3},{3,2},{4,5},{5,4},{6,7},{7,6},{8,9},{9,8},{10,11... | collective-permute-start | bytes 1769480 | tf_op jit(solution)/shard_map/ppermute | solution.py:559
  107.6 19.7 %collective-permute-start.23 = (bf16[16,2,128,128]{3,2,1,0:T(8,128)(2,1)S(1)}, bf16[16,2,128,128]{3,2,1,0:T(8,128)(2,1)S(1)}, u32[]{:S(2)}, u32[]{:S(2)}) collective-permute-start(bf16[16,2,128,128]{3,2,1,0:T(8,128)(2,1)S(1)} %get-tuple-element.51.env_ref), channel_id=1, source_target_pairs={{0,1},{2,3},{4,5},{6,7},{8,9},{10,11},{12,13},{14,15},{16,17},{18,... | collective-permute-start | bytes 3145736 | tf_op jit(solution)/shard_map/ppermute | solution.py:663
  108.9 22.6 %collective-permute-start.22 = (bf16[16,2,128,128]{3,2,1,0:T(8,128)(2,1)S(1)}, bf16[16,2,128,128]{3,2,1,0:T(8,128)(2,1)S(1)}, u32[]{:S(2)}, u32[]{:S(2)}) collective-permute-start(bf16[16,2,128,128]{3,2,1,0:T(8,128)(2,1)S(1)} %shard_map.76.refs_0_), channel_id=1, source_target_pairs={{1,8},{3,10},{5,12},{7,14},{9,24},{11,26},{13,28},{15,30},{17,0},{... | collective-permute-start | bytes 3145736 | tf_op jit(solution)/shard_map/ppermute | solution.py:660
  117.1 6.7 %collective-permute-start.10 = (bf16[6,128,128]{2,1,0:T(8,128)(2,1)S(1)}, bf16[6,128,128]{2,1,0:T(8,128)(2,1)S(1)}, u32[]{:S(2)}, u32[]{:S(2)}) collective-permute-start(bf16[6,128,128]{2,1,0:T(8,128)(2,1)S(1)} %shard_map.67), channel_id=1, source_target_pairs={{1,17},{3,19},{5,21},{7,23},{9,1},{11,3},{13,5},{15,7},{25,9},{27,... | collective-permute-start | bytes 589832 | tf_op jit(solution)/shard_map/ppermute | solution.py:594
  134.7 7.8 %collective-permute-start.24 = (bf16[4,2,128,128]{3,2,1,0:T(8,128)(2,1)S(1)}, bf16[4,2,128,128]{3,2,1,0:T(8,128)(2,1)S(1)}, u32[]{:S(2)}, u32[]{:S(2)}) collective-permute-start(bf16[4,2,128,128]{3,2,1,0:T(8,128)(2,1)S(1)} %shard_map.82), channel_id=1, source_target_pairs={{0,1},{2,3},{4,5},{6,7},{8,9},{10,11},{12,13},{14,15},{16,17},{18,... | collective-permute-start | bytes 786440 | tf_op jit(solution)/shard_map/ppermute | solution.py:699
  142.7 5.3 %collective-permute-start.25 = (bf16[2,2,128,128]{3,2,1,0:T(8,128)(2,1)S(1)}, bf16[2,2,128,128]{3,2,1,0:T(8,128)(2,1)S(1)}, u32[]{:S(2)}, u32[]{:S(2)}) collective-permute-start(bf16[2,2,128,128]{3,2,1,0:T(8,128)(2,1)S(1)} %get-tuple-element.58), channel_id=1, source_target_pairs={{0,1},{1,0},{2,3},{3,2},{4,5},{5,4},{6,7},{7,6},{8,9},{9,8},{10,11... | collective-permute-start | bytes 393224 | tf_op jit(solution)/shard_map/ppermute | solution.py:713
  144.5 5.0 %collective-permute-start.26 = (bf16[2,2,128,128]{3,2,1,0:T(8,128)(2,1)S(1)}, bf16[2,2,128,128]{3,2,1,0:T(8,128)(2,1)S(1)}, u32[]{:S(2)}, u32[]{:S(2)}) collective-permute-start(bf16[2,2,128,128]{3,2,1,0:T(8,128)(2,1)S(1)} %get-tuple-element.59), channel_id=1, source_target_pairs={{0,8},{1,9},{2,10},{3,11},{4,12},{5,13},{6,14},{7,15},{8,0},{9,1},... | collective-permute-start | bytes 393224 | tf_op jit(solution)/shard_map/ppermute | solution.py:713
  144.5 8.9 %collective-permute-start.27 = (bf16[2,2,128,128]{3,2,1,0:T(8,128)(2,1)S(1)}, bf16[2,2,128,128]{3,2,1,0:T(8,128)(2,1)S(1)}, u32[]{:S(2)}, u32[]{:S(2)}) collective-permute-start(bf16[2,2,128,128]{3,2,1,0:T(8,128)(2,1)S(1)} %get-tuple-element.60), channel_id=1, source_target_pairs={{0,9},{1,8},{2,11},{3,10},{4,13},{5,12},{6,15},{7,14},{8,1},{9,0},... | collective-permute-start | bytes 393224 | tf_op jit(solution)/shard_map/ppermute | solution.py:713
  146.2 7.2 %collective-permute-start.28 = (bf16[2,2,128,128]{3,2,1,0:T(8,128)(2,1)S(1)}, bf16[2,2,128,128]{3,2,1,0:T(8,128)(2,1)S(1)}, u32[]{:S(2)}, u32[]{:S(2)}) collective-permute-start(bf16[2,2,128,128]{3,2,1,0:T(8,128)(2,1)S(1)} %get-tuple-element.61), channel_id=1, source_target_pairs={{0,16},{1,17},{2,18},{3,19},{4,20},{5,21},{6,22},{7,23},{8,24},{9,... | collective-permute-start | bytes 393224 | tf_op jit(solution)/shard_map/ppermute | solution.py:713
  147.1 12.8 %collective-permute-start.29 = (bf16[2,2,128,128]{3,2,1,0:T(8,128)(2,1)S(1)}, bf16[2,2,128,128]{3,2,1,0:T(8,128)(2,1)S(1)}, u32[]{:S(2)}, u32[]{:S(2)}) collective-permute-start(bf16[2,2,128,128]{3,2,1,0:T(8,128)(2,1)S(1)} %get-tuple-element.62), channel_id=1, source_target_pairs={{0,17},{1,16},{2,19},{3,18},{4,21},{5,20},{6,23},{7,22},{8,25},{9,... | collective-permute-start | bytes 393224 | tf_op jit(solution)/shard_map/ppermute | solution.py:713
  148.0 11.9 %collective-permute-start.30 = (bf16[2,2,128,128]{3,2,1,0:T(8,128)(2,1)S(1)}, bf16[2,2,128,128]{3,2,1,0:T(8,128)(2,1)S(1)}, u32[]{:S(2)}, u32[]{:S(2)}) collective-permute-start(bf16[2,2,128,128]{3,2,1,0:T(8,128)(2,1)S(1)} %get-tuple-element.63), channel_id=1, source_target_pairs={{0,24},{1,25},{2,26},{3,27},{4,28},{5,29},{6,30},{7,31},{8,16},{9,... | collective-permute-start | bytes 393224 | tf_op jit(solution)/shard_map/ppermute | solution.py:713
  149.5 10.4 %collective-permute-start.31 = (bf16[2,2,128,128]{3,2,1,0:T(8,128)(2,1)S(1)}, bf16[2,2,128,128]{3,2,1,0:T(8,128)(2,1)S(1)}, u32[]{:S(2)}, u32[]{:S(2)}) collective-permute-start(bf16[2,2,128,128]{3,2,1,0:T(8,128)(2,1)S(1)} %get-tuple-element.64), channel_id=1, source_target_pairs={{0,25},{1,24},{2,27},{3,26},{4,29},{5,28},{6,31},{7,30},{8,17},{9,... | collective-permute-start | bytes 393224 | tf_op jit(solution)/shard_map/ppermute | solution.py:713
  (22 other events, 270.6 us)
where the time goes:
time: 162 us; the launch traced here: 161 us
  starting transfers between devices  56.1 us (35%)
  waiting for transfers between devices  51.4 us (32%)
  Pallas kernels  38.5 us (24%)
  local copies, waits for them, and re-layouts  14.6 us (9%)
    pallas_call x21, Pallas kernels, plain_call(): pl.pallas_call(kernel, out_shape=out_shape, in_specs=specs, out_specs=pla...  38.5 us
    ppermute x3, waiting for transfers between devices, sweep(): lax.ppermute(packed, 'op', [(o, o ^ hop) for o in range(op_count)])  22.4 us
    ppermute x3, starting transfers between devices, sweep(): lax.ppermute(matrix, 'chain', [(c, c ^ hop) for c in range(chain_count)])  14.1 us
    unnamed x45, local copies, waits for them, and re-layouts  13.5 us
    ppermute x2, starting transfers between devices, sweep(): outside = lax.ppermute(leaving, both, outer_halo)  11.7 us
    ppermute x3, waiting for transfers between devices, sweep(): lax.ppermute(matrix, 'chain', [(c, c ^ hop) for c in range(chain_count)])  11.7 us
    ppermute x7, waiting for transfers between devices, sweep(): lax.ppermute(piece, both, [(flat(c, o), flat(c ^ hop, o ^ turn)) for c, o...  9.61 us
    ppermute x7, starting transfers between devices, sweep(): lax.ppermute(piece, both, [(flat(c, o), flat(c ^ hop, o ^ turn)) for c, o...  7.54 us
  transfers between devices with their start and end apart: 32, of which 12 were waited for; matrix products, arithmetic and copies ran while one was open for 1% of the time, Pallas kernels for 19%

commit v1 on v0

--- a/solution.py
+++ b/solution.py
@@ -370,25 +370,42 @@
     keep_ref[...] = out_ref[pl.ds(lax.axis_index("op") // spread * count, count)]
 
 
+def finish_whole(row, bond, charges, turned, kron, flat, deep, summed, out_ref):
+    step = bond * GROUP
+    level = jnp.concatenate([kron[:, :step], kron[:, 2 * step : 3 * step]], axis=1)
+    for down, (mixed, left) in enumerate(((flat, level), (deep, kron[...]))):
+
+        def store(at, low, high):
+            summed[:, pl.ds(at, GROUP), :] = low
+            summed[:, pl.ds(at + GROUP, GROUP), :] = high
+
+        def write(index, value):
+            out_ref[index, down] = value.astype(jnp.bfloat16)
+
+        contract(mixed, left, store)
+        project(down, row, bond, 0, charges, turned, summed, write)
+
+
 def first_kernel(chain_count, spread, bond, chunks, charges, mps_ref, turned, kron, *refs):
     env_refs, (out_ref, keep_ref, flat, deep, summed) = refs[:chunks], refs[chunks:]
     row = my_row(chain_count, spread)
     mix(env_refs, 0, mps_ref, spread, bond, flat, deep, 0, 0)
     mix(env_refs, -1, mps_ref, spread, bond, flat, deep, bond, 2 * bond)
-    step = bond * GROUP
-    level = jnp.concatenate([kron[:, :step], kron[:, 2 * step : 3 * step]], axis=1)
-    for down, (mixed, left) in enumerate(((flat, level), (deep, kron[...]))):
-
-        def store(at, low, high):
-            summed[:, pl.ds(at, GROUP), :] = low
-            summed[:, pl.ds(at + GROUP, GROUP), :] = high
-
-        def write(index, value):
-            out_ref[index, down] = value.astype(jnp.bfloat16)
-
-        contract(mixed, left, store)
-        project(down, row, bond, 0, charges, turned, summed, write)
+    finish_whole(row, bond, charges, turned, kron, flat, deep, summed, out_ref)
     keep_part(spread, out_ref, keep_ref)
+
+
+def inner_kernel(
+    chain_count, spread, bond, charges, mps_ref, turned, kron, env_ref, inside_ref, out_ref,
+    flat, deep, summed
+):
+    row = my_row(chain_count, spread)
+
+    @pl.when(lax.rem(lax.axis_index("op"), spread) != 0)
+    def _():
+        mix([env_ref], 0, mps_ref, spread, bond, flat, deep, 0, 0)
+        mix([inside_ref], -1, mps_ref, spread, bond, flat, deep, bond, 2 * bond)
+        finish_whole(row, bond, charges, turned, kron, flat, deep, summed, out_ref)
 
 
 def main_kernel(
@@ -663,6 +680,19 @@
                 inside = lax.ppermute(finished, both, inner_halo)
                 passed.append(
                     call(
+                        functools.partial(inner_kernel, chain_count, spread, bond),
+                        full[0],
+                        [SMEM] + [VMEM] * 5,
+                        shared[:-1] + [finished, inside],
+                        [
+                            pltpu.VMEM((2 * bond, *square), jnp.float32),
+                            pltpu.VMEM((4 * bond, *square), jnp.float32),
+                            pltpu.VMEM((pairs, *square), jnp.float32),
+                        ],
+                        limit=28,
+                    )
+                    if site == 1
+                    else call(
                         functools.partial(main_kernel, chain_count, spread, bond, False),
                         full[0],
                         [SMEM] + [VMEM] * 5,

time: 162 us -> 169 us (1.043)
  the two profiles are of different devices: /device:TPU:27 before, /device:TPU:15 now
where the time goes in v1:
time: 169 us
  starting transfers between devices  58.1 us (34%)
  waiting for transfers between devices  55.4 us (33%)
  Pallas kernels  40 us (24%)
  local copies, waits for them, and re-layouts  14.6 us (9%)
    pallas_call x21, Pallas kernels, plain_call(): pl.pallas_call(kernel, out_shape=out_shape, in_specs=specs, out_specs=pla...  40 us
    ppermute x3, waiting for transfers between devices, sweep(): lax.ppermute(packed, 'op', [(o, o ^ hop) for o in range(op_count)])  27.4 us
    ppermute x3, starting transfers between devices, sweep(): lax.ppermute(matrix, 'chain', [(c, c ^ hop) for c in range(chain_count)])  14.9 us
    unnamed x45, local copies, waits for them, and re-layouts  13.5 us
    ppermute x1, starting transfers between devices, sweep(): lax.ppermute(extra, both, [(flat(ring_chain(at + 1, chain_count), o), fla...  12.6 us
    ppermute x3, waiting for transfers between devices, sweep(): lax.ppermute(matrix, 'chain', [(c, c ^ hop) for c in range(chain_count)])  11.7 us
    ppermute x7, waiting for transfers between devices, sweep(): lax.ppermute(piece, both, [(flat(c, o), flat(c ^ hop, o ^ turn)) for c, o...  10.7 us
    ppermute x7, starting transfers between devices, sweep(): lax.ppermute(piece, both, [(flat(c, o), flat(c ^ hop, o ^ turn)) for c, o...  9.45 us
  transfers between devices with their start and end apart: 32, of which 11 were waited for; matrix products, arithmetic and copies ran while one was open for 1% of the time, Pallas kernels for 19%

profile of v1, /device:TPU:15, one launch (start us, length us, event | category | flops | bytes accessed | tf_op | source)
XLA Modules:
  0.0 168.5 jit_solution(15580756515445852167)
XLA Ops:
  0.0 3.0 %shard_map.66 = (bf16[18,128,128]{2,1,0:T(8,128)(2,1)}, bf16[18,128,128]{2,1,0:T(8,128)(2,1)}, bf16[18,128,128]{2,1,0:T(8,128)(2,1)}) custom-call(bf16[1,4,16,128,128]{4,3,2,1,0:T(8,128)(2,1)} %mps_ref.3, bf16[1,4,8,2,128,128]{5,4,3,2,1,0:T(8,128)(2,1)} %bitcast.5), custom_call_target="tpu_custom_call" | custom-call | flops 100000000 | bytes 1000000 | tf_op jit(solution)/shard_map/pallas_call | solution.py:77
  4.8 1.9 %shard_map.73 = bf16[2,3,2,128,128]{4,3,2,1,0:T(8,128)(2,1)} custom-call(bf16[2,8,2,128,128]{4,3,2,1,0:T(8,128)(2,1)} %bitcast.7), custom_call_target="tpu_custom_call" | custom-call | flops 100000000 | bytes 1000000 | tf_op jit(solution)/shard_map/pallas_call | solution.py:77
  7.9 1.6 collective-permute-start
  9.5 8.4 %collective-permute-done.refs_1_ = bf16[64,128]{1,0:T(8,128)(2,1)S(1)} collective-permute-done((bf16[64,128]{1,0:T(8,128)(2,1)S(1)}, bf16[64,128]{1,0:T(8,128)(2,1)S(1)}, u32[]{:S(2)}, u32[]{:S(2)}) %collective-permute-start) | collective-permute-done | bytes 16416 | tf_op jit(solution)/shard_map/ppermute | solution.py:585
  18.5 12.5 %collective-permute-start.1 = (bf16[64,128]{1,0:T(8,128)(2,1)S(1)}, bf16[64,128]{1,0:T(8,128)(2,1)S(1)}, u32[]{:S(2)}, u32[]{:S(2)}) collective-permute-start(bf16[64,128]{1,0:T(8,128)(2,1)S(1)} %pad.4.refs_0_), channel_id=1, source_target_pairs={{0,16},{8,24},{16,0},{24,8},{1,17},{9,25},{17,1},{25,9},{2,18},{10... | collective-permute-start | bytes 49160 | tf_op jit(solution)/shard_map/ppermute | solution.py:585
  34.1 2.2 %collective-permute-done.2.refs_3_ = bf16[64,128]{1,0:T(8,128)(2,1)S(1)} collective-permute-done((bf16[64,128]{1,0:T(8,128)(2,1)S(1)}, bf16[64,128]{1,0:T(8,128)(2,1)S(1)}, u32[]{:S(2)}, u32[]{:S(2)}) %collective-permute-start.2) | collective-permute-done | bytes 16416 | tf_op jit(solution)/shard_map/ppermute | solution.py:585
  36.8 2.3 %collective-permute-start.16 = (bf16[2,3,2,128,128]{4,3,2,1,0:T(8,128)(2,1)}, bf16[2,3,2,128,128]{4,3,2,1,0:T(8,128)(2,1)}, u32[]{:S(2)}, u32[]{:S(2)}) collective-permute-start(bf16[2,3,2,128,128]{4,3,2,1,0:T(8,128)(2,1)} %shard_map.73), channel_id=1, source_target_pairs={{0,4},{1,5},{2,6},{3,7},{4,0},{5,1},{6,2},{7,3},{8,12},{9,13},{10,... | collective-permute-start | bytes 1179656 | tf_op jit(solution)/shard_map/ppermute | solution.py:534
  39.2 1.6 copy-done.3
  40.7 1.6 copy-done.4
  42.9 4.2 %collective-permute-start.3 = (bf16[18,128,128]{2,1,0:T(8,128)(2,1)S(1)}, bf16[18,128,128]{2,1,0:T(8,128)(2,1)S(1)}, u32[]{:S(2)}, u32[]{:S(2)}) collective-permute-start(bf16[18,128,128]{2,1,0:T(8,128)(2,1)S(1)} %shard_map.65.refs_0_.refs_4_), channel_id=1, source_target_pairs={{0,1},{1,0},{2,3},{3,2},{4,5},{5,4},{6,7},{7,6},{8,9},{9,8},{10,11... | collective-permute-start | bytes 1769480 | tf_op jit(solution)/shard_map/ppermute | solution.py:576
  47.6 9.0 %collective-permute-done.16.refs_4_ = bf16[2,3,2,128,128]{4,3,2,1,0:T(8,128)(2,1)} collective-permute-done((bf16[2,3,2,128,128]{4,3,2,1,0:T(8,128)(2,1)}, bf16[2,3,2,128,128]{4,3,2,1,0:T(8,128)(2,1)}, u32[]{:S(2)}, u32[]{:S(2)}) %collective-permute-start.16) | collective-permute-done | bytes 393248 | tf_op jit(solution)/shard_map/ppermute | solution.py:534
  57.1 18.4 %collective-permute-done.18.refs_6_ = bf16[2,3,2,128,128]{4,3,2,1,0:T(8,128)(2,1)} collective-permute-done((bf16[2,3,2,128,128]{4,3,2,1,0:T(8,128)(2,1)}, bf16[2,3,2,128,128]{4,3,2,1,0:T(8,128)(2,1)}, u32[]{:S(2)}, u32[]{:S(2)}) %collective-permute-start.18) | collective-permute-done | bytes 393248 | tf_op jit(solution)/shard_map/ppermute | solution.py:534
  79.1 2.7 %collective-permute-start.8 = (bf16[18,128,128]{2,1,0:T(8,128)(2,1)}, bf16[18,128,128]{2,1,0:T(8,128)(2,1)S(1)}, u32[]{:S(2)}, u32[]{:S(2)}) collective-permute-start(bf16[18,128,128]{2,1,0:T(8,128)(2,1)} %get-tuple-element.37), channel_id=1, source_target_pairs={{8,16},{16,8},{24,0},{9,17},{17,9},{25,1},{10,18},{18,10},{26,2},{... | collective-permute-start | bytes 1769480 | tf_op jit(solution)/shard_map/ppermute | solution.py:569
  89.5 2.2 %shard_map.71 = (bf16[6,128,128]{2,1,0:T(8,128)(2,1)S(1)}, bf16[7,128,512]{2,1,0:T(8,128)(2,1)S(1)}, bf16[512,512]{1,0:T(8,128)(2,1)S(1)}) custom-call(s32[5,16]{1,0:T(8,128)S(1)} %copy-done.20, f32[64,128]{1,0:T(8,128)S(1)} %shard_map.64.mask, bf16[64,128]{1,0:T(8,128)(2,1)S(1)} %copy-done.9, bf16[64,128]{1,0:T(8,128)(2,1)S(1)} %copy-done.12, ...), custom_call_target="tpu_custom_call" | custom-call | flops 100000000 | bytes 1000000 | tf_op jit(solution)/shard_map/pallas_call | solution.py:77
  91.7 5.8 %shard_map.74 = (bf16[16,2,128,128]{3,2,1,0:T(8,128)(2,1)S(1)}, bf16[4,2,128,128]{3,2,1,0:T(8,128)(2,1)S(1)}) custom-call(s32[16,2]{1,0:T(8,128)S(1)} %copy.14.charges, bf16[6,128,128]{2,1,0:T(8,128)(2,1)S(1)} %get-tuple-element.47.mps_ref, bf16[7,128,512]{2,1,0:T(8,128)(2,1)S(1)} %get-tuple-element.48.turned, bf16[512,512]{1,0:T(8,128)(2,1)S(1)} %get-tuple-element.49.kron, ...), custom_call_target="tpu_custom_call" | custom-call | flops 100000000 | bytes 1000000 | tf_op jit(solution)/shard_map/pallas_call | solution.py:77
  99.6 1.8 %collective-permute-start.9 = (bf16[18,128,128]{2,1,0:T(8,128)(2,1)S(1)}, bf16[18,128,128]{2,1,0:T(8,128)(2,1)S(1)}, u32[]{:S(2)}, u32[]{:S(2)}) collective-permute-start(bf16[18,128,128]{2,1,0:T(8,128)(2,1)S(1)} %collective-permute-done.8.refs_3_.refs_10_), channel_id=1, source_target_pairs={{0,1},{1,0},{2,3},{3,2},{4,5},{5,4},{6,7},{7,6},{8,9},{9,8},{10,11... | collective-permute-start | bytes 1769480 | tf_op jit(solution)/shard_map/ppermute | solution.py:576
  101.4 1.6 collective-permute-done.9.refs_11_
  104.4 2.0 %shard_map.75.own_ref = f32[2,64,128,128]{3,2,1,0:T(8,128)S(1)} custom-call(bf16[6,128,128]{2,1,0:T(8,128)(2,1)S(1)} %get-tuple-element.44.mps_ref, bf16[512,512]{1,0:T(8,128)(2,1)S(1)} %get-tuple-element.46.kron, bf16[16,2,128,128]{3,2,1,0:T(8,128)(2,1)S(1)} %get-tuple-element.50.env_ref), custom_call_target="tpu_custom_call" | custom-call | flops 100000000 | bytes 1000000 | tf_op jit(solution)/shard_map/pallas_call | solution.py:77
  106.5 4.9 %shard_map.76.refs_0_ = bf16[16,2,128,128]{3,2,1,0:T(8,128)(2,1)S(1)} custom-call(s32[16,2]{1,0:T(8,128)S(1)} %copy.14.charges, bf16[6,128,128]{2,1,0:T(8,128)(2,1)S(1)} %get-tuple-element.44.mps_ref, bf16[7,128,512]{2,1,0:T(8,128)(2,1)S(1)} %get-tuple-element.45.turned, bf16[512,512]{1,0:T(8,128)(2,1)S(1)} %get-tuple-element.46.kron, ...), custom_call_target="tpu_custom_call" | custom-call | flops 100000000 | bytes 1000000 | tf_op jit(solution)/shard_map/pallas_call | solution.py:77
  114.5 12.6 %collective-permute-start.10 = (bf16[6,128,128]{2,1,0:T(8,128)(2,1)S(1)}, bf16[6,128,128]{2,1,0:T(8,128)(2,1)S(1)}, u32[]{:S(2)}, u32[]{:S(2)}) collective-permute-start(bf16[6,128,128]{2,1,0:T(8,128)(2,1)S(1)} %shard_map.67), channel_id=1, source_target_pairs={{1,17},{3,19},{5,21},{7,23},{9,1},{11,3},{13,5},{15,7},{25,9},{27,... | collective-permute-start | bytes 589832 | tf_op jit(solution)/shard_map/ppermute | solution.py:611
  129.8 1.5 shard_map.68
  131.2 2.0 %shard_map.78.own_ref = f32[2,64,128,128]{3,2,1,0:T(8,128)S(1)} custom-call(bf16[6,128,128]{2,1,0:T(8,128)(2,1)S(1)} %get-tuple-element.41.mps_ref, bf16[512,512]{1,0:T(8,128)(2,1)S(1)} %get-tuple-element.43.kron, bf16[16,2,128,128]{3,2,1,0:T(8,128)(2,1)S(1)} %get-tuple-element.51.env_ref), custom_call_target="tpu_custom_call" | custom-call | flops 100000000 | bytes 1000000 | tf_op jit(solution)/shard_map/pallas_call | solution.py:77
  133.3 4.2 %shard_map.79.refs_0_ = bf16[16,2,128,128]{3,2,1,0:T(8,128)(2,1)S(1)} custom-call(s32[16,2]{1,0:T(8,128)S(1)} %copy.14.charges, bf16[6,128,128]{2,1,0:T(8,128)(2,1)S(1)} %get-tuple-element.41.mps_ref, bf16[7,128,512]{2,1,0:T(8,128)(2,1)S(1)} %get-tuple-element.42.turned, bf16[512,512]{1,0:T(8,128)(2,1)S(1)} %get-tuple-element.43.kron, ...), custom_call_target="tpu_custom_call" | custom-call | flops 100000000 | bytes 1000000 | tf_op jit(solution)/shard_map/pallas_call | solution.py:77
  138.3 2.4 %shard_map.82 = bf16[4,2,128,128]{3,2,1,0:T(8,128)(2,1)S(1)} custom-call(s32[16,2]{1,0:T(8,128)S(1)} %copy.14.charges, bf16[6,128,128]{2,1,0:T(8,128)(2,1)S(1)} %get-tuple-element.38.mps_ref, bf16[7,128,512]{2,1,0:T(8,128)(2,1)S(1)} %get-tuple-element.53.turned, bf16[512,512]{1,0:T(8,128)(2,1)S(1)} %get-tuple-element.40.kron, ...), custom_call_target="tpu_custom_call" | custom-call | flops 100000000 | bytes 1000000 | tf_op jit(solution)/shard_map/pallas_call | solution.py:77
  142.0 2.4 %shard_map.81.own_ref = f32[4,2,128,128]{3,2,1,0:T(8,128)S(1)} custom-call(s32[16,2]{1,0:T(8,128)S(1)} %copy.14.charges, bf16[6,128,128]{2,1,0:T(8,128)(2,1)S(1)} %get-tuple-element.38.mps_ref, bf16[7,128,512]{2,1,0:T(8,128)(2,1)S(1)} %get-tuple-element.39.turned, bf16[512,512]{1,0:T(8,128)(2,1)S(1)} %get-tuple-element.40.kron, ...), custom_call_target="tpu_custom_call" | custom-call | flops 100000000 | bytes 1000000 | tf_op jit(solution)/shard_map/pallas_call | solution.py:77
  144.3 2.7 %collective-permute-done.24.before_ref = bf16[4,2,128,128]{3,2,1,0:T(8,128)(2,1)S(1)} collective-permute-done((bf16[4,2,128,128]{3,2,1,0:T(8,128)(2,1)S(1)}, bf16[4,2,128,128]{3,2,1,0:T(8,128)(2,1)S(1)}, u32[]{:S(2)}, u32[]{:S(2)}) %collective-permute-start.24) | collective-permute-done | bytes 262176 | tf_op jit(solution)/shard_map/ppermute | solution.py:729
  147.3 4.8 %collective-permute-start.25 = (bf16[2,2,128,128]{3,2,1,0:T(8,128)(2,1)S(1)}, bf16[2,2,128,128]{3,2,1,0:T(8,128)(2,1)S(1)}, u32[]{:S(2)}, u32[]{:S(2)}) collective-permute-start(bf16[2,2,128,128]{3,2,1,0:T(8,128)(2,1)S(1)} %get-tuple-element.58), channel_id=1, source_target_pairs={{0,1},{1,0},{2,3},{3,2},{4,5},{5,4},{6,7},{7,6},{8,9},{9,8},{10,11... | collective-permute-start | bytes 393224 | tf_op jit(solution)/shard_map/ppermute | solution.py:743
  152.1 1.7 %collective-permute-start.27 = (bf16[2,2,128,128]{3,2,1,0:T(8,128)(2,1)S(1)}, bf16[2,2,128,128]{3,2,1,0:T(8,128)(2,1)S(1)}, u32[]{:S(2)}, u32[]{:S(2)}) collective-permute-start(bf16[2,2,128,128]{3,2,1,0:T(8,128)(2,1)S(1)} %get-tuple-element.60), channel_id=1, source_target_pairs={{0,9},{1,8},{2,11},{3,10},{4,13},{5,12},{6,15},{7,14},{8,1},{9,0},... | collective-permute-start | bytes 393224 | tf_op jit(solution)/shard_map/ppermute | solution.py:743
  153.8 1.8 %collective-permute-start.29 = (bf16[2,2,128,128]{3,2,1,0:T(8,128)(2,1)S(1)}, bf16[2,2,128,128]{3,2,1,0:T(8,128)(2,1)S(1)}, u32[]{:S(2)}, u32[]{:S(2)}) collective-permute-start(bf16[2,2,128,128]{3,2,1,0:T(8,128)(2,1)S(1)} %get-tuple-element.62), channel_id=1, source_target_pairs={{0,17},{1,16},{2,19},{3,18},{4,21},{5,20},{6,23},{7,22},{8,25},{9,... | collective-permute-start | bytes 393224 | tf_op jit(solution)/shard_map/ppermute | solution.py:743
  155.6 1.5 collective-permute-done.26.refs_2_
  158.2 2.8 %collective-permute-done.27.refs_3_ = bf16[2,2,128,128]{3,2,1,0:T(8,128)(2,1)S(1)} collective-permute-done((bf16[2,2,128,128]{3,2,1,0:T(8,128)(2,1)S(1)}, bf16[2,2,128,128]{3,2,1,0:T(8,128)(2,1)S(1)}, u32[]{:S(2)}, u32[]{:S(2)}) %collective-permute-start.27) | collective-permute-done | bytes 131104 | tf_op jit(solution)/shard_map/ppermute | solution.py:743
  161.0 6.5 %collective-permute-done.29.refs_5_ = bf16[2,2,128,128]{3,2,1,0:T(8,128)(2,1)S(1)} collective-permute-done((bf16[2,2,128,128]{3,2,1,0:T(8,128)(2,1)S(1)}, bf16[2,2,128,128]{3,2,1,0:T(8,128)(2,1)S(1)}, u32[]{:S(2)}, u32[]{:S(2)}) %collective-permute-start.29) | collective-permute-done | bytes 131104 | tf_op jit(solution)/shard_map/ppermute | solution.py:743
  (103 shorter events, 33.7 us)
Async XLA Ops:
  3.0 44.2 %collective-permute-start.4 = (bf16[18,128,128]{2,1,0:T(8,128)(2,1)}, bf16[18,128,128]{2,1,0:T(8,128)(2,1)S(1)}, u32[]{:S(2)}, u32[]{:S(2)}) collective-permute-start(bf16[18,128,128]{2,1,0:T(8,128)(2,1)} %get-tuple-element.35), channel_id=1, source_target_pairs={{0,8},{8,0},{16,24},{24,16},{1,9},{9,1},{17,25},{25,17},{2,10},{10... | collective-permute-start | bytes 1769480 | tf_op jit(solution)/shard_map/ppermute | solution.py:565
  3.3 43.9 %collective-permute-start.6 = (bf16[18,128,128]{2,1,0:T(8,128)(2,1)}, bf16[18,128,128]{2,1,0:T(8,128)(2,1)S(1)}, u32[]{:S(2)}, u32[]{:S(2)}) collective-permute-start(bf16[18,128,128]{2,1,0:T(8,128)(2,1)} %get-tuple-element.36), channel_id=1, source_target_pairs={{0,16},{8,24},{16,0},{24,8},{1,17},{9,25},{17,1},{25,9},{2,18},{10... | collective-permute-start | bytes 1769480 | tf_op jit(solution)/shard_map/ppermute | solution.py:565
  3.5 53.1 %collective-permute-start.11 = (bf16[18,128,128]{2,1,0:T(8,128)(2,1)}, bf16[18,128,128]{2,1,0:T(8,128)(2,1)}, u32[]{:S(2)}, u32[]{:S(2)}) collective-permute-start(bf16[18,128,128]{2,1,0:T(8,128)(2,1)} %get-tuple-element.37), channel_id=1, source_target_pairs={{0,24},{1,25},{2,26},{3,27},{4,28},{5,29},{6,30},{7,31}} | collective-permute-start | bytes 1769480 | tf_op jit(solution)/shard_map/ppermute | solution.py:567
  6.7 36.3 %collective-permute-start.14 = (bf16[2,3,2,128,128]{4,3,2,1,0:T(8,128)(2,1)}, bf16[2,3,2,128,128]{4,3,2,1,0:T(8,128)(2,1)}, u32[]{:S(2)}, u32[]{:S(2)}) collective-permute-start(bf16[2,3,2,128,128]{4,3,2,1,0:T(8,128)(2,1)} %shard_map.73), channel_id=1, source_target_pairs={{0,2},{1,3},{2,0},{3,1},{4,6},{5,7},{6,4},{7,5},{8,10},{9,11},{10,... | collective-permute-start | bytes 1179656 | tf_op jit(solution)/shard_map/ppermute | solution.py:534
  7.9 10.0 %collective-permute-start = (bf16[64,128]{1,0:T(8,128)(2,1)S(1)}, bf16[64,128]{1,0:T(8,128)(2,1)S(1)}, u32[]{:S(2)}, u32[]{:S(2)}) collective-permute-start(bf16[64,128]{1,0:T(8,128)(2,1)S(1)} %pad.4.refs_0_), channel_id=1, source_target_pairs={{0,8},{8,0},{16,24},{24,16},{1,9},{9,1},{17,25},{25,17},{2,10},{10... | collective-permute-start | bytes 49160 | tf_op jit(solution)/shard_map/ppermute | solution.py:585
  18.5 13.6 %collective-permute-start.1 = (bf16[64,128]{1,0:T(8,128)(2,1)S(1)}, bf16[64,128]{1,0:T(8,128)(2,1)S(1)}, u32[]{:S(2)}, u32[]{:S(2)}) collective-permute-start(bf16[64,128]{1,0:T(8,128)(2,1)S(1)} %pad.4.refs_0_), channel_id=1, source_target_pairs={{0,16},{8,24},{16,0},{24,8},{1,17},{9,25},{17,1},{25,9},{2,18},{10... | collective-permute-start | bytes 49160 | tf_op jit(solution)/shard_map/ppermute | solution.py:585
  32.8 3.5 %collective-permute-start.2 = (bf16[64,128]{1,0:T(8,128)(2,1)S(1)}, bf16[64,128]{1,0:T(8,128)(2,1)S(1)}, u32[]{:S(2)}, u32[]{:S(2)}) collective-permute-start(bf16[64,128]{1,0:T(8,128)(2,1)S(1)} %pad.4.refs_0_), channel_id=1, source_target_pairs={{0,24},{8,16},{16,8},{24,0},{1,25},{9,17},{17,9},{25,1},{2,26},{10... | collective-permute-start | bytes 49160 | tf_op jit(solution)/shard_map/ppermute | solution.py:585
  36.8 19.8 %collective-permute-start.16 = (bf16[2,3,2,128,128]{4,3,2,1,0:T(8,128)(2,1)}, bf16[2,3,2,128,128]{4,3,2,1,0:T(8,128)(2,1)}, u32[]{:S(2)}, u32[]{:S(2)}) collective-permute-start(bf16[2,3,2,128,128]{4,3,2,1,0:T(8,128)(2,1)} %shard_map.73), channel_id=1, source_target_pairs={{0,4},{1,5},{2,6},{3,7},{4,0},{5,1},{6,2},{7,3},{8,12},{9,13},{10,... | collective-permute-start | bytes 1179656 | tf_op jit(solution)/shard_map/ppermute | solution.py:534
  42.9 34.0 %collective-permute-start.3 = (bf16[18,128,128]{2,1,0:T(8,128)(2,1)S(1)}, bf16[18,128,128]{2,1,0:T(8,128)(2,1)S(1)}, u32[]{:S(2)}, u32[]{:S(2)}) collective-permute-start(bf16[18,128,128]{2,1,0:T(8,128)(2,1)S(1)} %shard_map.65.refs_0_.refs_4_), channel_id=1, source_target_pairs={{0,1},{1,0},{2,3},{3,2},{4,5},{5,4},{6,7},{7,6},{8,9},{9,8},{10,11... | collective-permute-start | bytes 1769480 | tf_op jit(solution)/shard_map/ppermute | solution.py:576
  47.1 29.8 %collective-permute-start.5 = (bf16[18,128,128]{2,1,0:T(8,128)(2,1)S(1)}, bf16[18,128,128]{2,1,0:T(8,128)(2,1)S(1)}, u32[]{:S(2)}, u32[]{:S(2)}) collective-permute-start(bf16[18,128,128]{2,1,0:T(8,128)(2,1)S(1)} %collective-permute-done.4.refs_1_.refs_6_), channel_id=1, source_target_pairs={{0,1},{1,0},{2,3},{3,2},{4,5},{5,4},{6,7},{7,6},{8,9},{9,8},{10,11... | collective-permute-start | bytes 1769480 | tf_op jit(solution)/shard_map/ppermute | solution.py:576
  47.2 30.2 %collective-permute-start.7 = (bf16[18,128,128]{2,1,0:T(8,128)(2,1)S(1)}, bf16[18,128,128]{2,1,0:T(8,128)(2,1)S(1)}, u32[]{:S(2)}, u32[]{:S(2)}) collective-permute-start(bf16[18,128,128]{2,1,0:T(8,128)(2,1)S(1)} %collective-permute-done.6.refs_2_.refs_8_), channel_id=1, source_target_pairs={{0,1},{1,0},{2,3},{3,2},{4,5},{5,4},{6,7},{7,6},{8,9},{9,8},{10,11... | collective-permute-start | bytes 1769480 | tf_op jit(solution)/shard_map/ppermute | solution.py:576
  56.6 18.9 %collective-permute-start.18 = (bf16[2,3,2,128,128]{4,3,2,1,0:T(8,128)(2,1)}, bf16[2,3,2,128,128]{4,3,2,1,0:T(8,128)(2,1)}, u32[]{:S(2)}, u32[]{:S(2)}) collective-permute-start(bf16[2,3,2,128,128]{4,3,2,1,0:T(8,128)(2,1)} %shard_map.73), channel_id=1, source_target_pairs={{0,6},{1,7},{2,4},{3,5},{4,2},{5,3},{6,0},{7,1},{8,14},{9,15},{10,... | collective-permute-start | bytes 1179656 | tf_op jit(solution)/shard_map/ppermute | solution.py:534
  56.6 21.7 %collective-permute-start.12 = (bf16[18,128,128]{2,1,0:T(8,128)(2,1)}, bf16[18,128,128]{2,1,0:T(8,128)(2,1)S(1)}, u32[]{:S(2)}, u32[]{:S(2)}) collective-permute-start(bf16[18,128,128]{2,1,0:T(8,128)(2,1)} %collective-permute-done.11.refs_10_), channel_id=1, source_target_pairs={{0,1},{1,0},{2,3},{3,2},{4,5},{5,4},{6,7},{7,6},{8,9},{9,8},{10,11... | collective-permute-start | bytes 1769480 | tf_op jit(solution)/shard_map/ppermute | solution.py:576
  75.5 16.1 %collective-permute-start.13 = (bf16[2,3,2,128,128]{4,3,2,1,0:T(8,128)(2,1)}, bf16[2,3,2,128,128]{4,3,2,1,0:T(8,128)(2,1)}, u32[]{:S(2)}, u32[]{:S(2)}) collective-permute-start(bf16[2,3,2,128,128]{4,3,2,1,0:T(8,128)(2,1)} %shard_map.73), channel_id=1, source_target_pairs={{0,1},{1,0},{2,3},{3,2},{4,5},{5,4},{6,7},{7,6},{8,9},{9,8},{10,11... | collective-permute-start | bytes 1179656 | tf_op jit(solution)/shard_map/ppermute | solution.py:539
  76.9 14.8 %collective-permute-start.15 = (bf16[2,3,2,128,128]{4,3,2,1,0:T(8,128)(2,1)}, bf16[2,3,2,128,128]{4,3,2,1,0:T(8,128)(2,1)}, u32[]{:S(2)}, u32[]{:S(2)}) collective-permute-start(bf16[2,3,2,128,128]{4,3,2,1,0:T(8,128)(2,1)} %collective-permute-done.14.refs_2_), channel_id=1, source_target_pairs={{0,1},{1,0},{2,3},{3,2},{4,5},{5,4},{6,7},{7,6},{8,9},{9,8},{10,11... | collective-permute-start | bytes 1179656 | tf_op jit(solution)/shard_map/ppermute | solution.py:539
  76.9 14.8 %collective-permute-start.17 = (bf16[2,3,2,128,128]{4,3,2,1,0:T(8,128)(2,1)}, bf16[2,3,2,128,128]{4,3,2,1,0:T(8,128)(2,1)}, u32[]{:S(2)}, u32[]{:S(2)}) collective-permute-start(bf16[2,3,2,128,128]{4,3,2,1,0:T(8,128)(2,1)} %collective-permute-done.16.refs_4_), channel_id=1, source_target_pairs={{0,1},{1,0},{2,3},{3,2},{4,5},{5,4},{6,7},{7,6},{8,9},{9,8},{10,11... | collective-permute-start | bytes 1179656 | tf_op jit(solution)/shard_map/ppermute | solution.py:539
  78.2 13.5 %collective-permute-start.19 = (bf16[2,3,2,128,128]{4,3,2,1,0:T(8,128)(2,1)}, bf16[2,3,2,128,128]{4,3,2,1,0:T(8,128)(2,1)}, u32[]{:S(2)}, u32[]{:S(2)}) collective-permute-start(bf16[2,3,2,128,128]{4,3,2,1,0:T(8,128)(2,1)} %collective-permute-done.18.refs_6_), channel_id=1, source_target_pairs={{0,1},{1,0},{2,3},{3,2},{4,5},{5,4},{6,7},{7,6},{8,9},{9,8},{10,11... | collective-permute-start | bytes 1179656 | tf_op jit(solution)/shard_map/ppermute | solution.py:539
  79.1 20.5 %collective-permute-start.8 = (bf16[18,128,128]{2,1,0:T(8,128)(2,1)}, bf16[18,128,128]{2,1,0:T(8,128)(2,1)S(1)}, u32[]{:S(2)}, u32[]{:S(2)}) collective-permute-start(bf16[18,128,128]{2,1,0:T(8,128)(2,1)} %get-tuple-element.37), channel_id=1, source_target_pairs={{8,16},{16,8},{24,0},{9,17},{17,9},{25,1},{10,18},{18,10},{26,2},{... | collective-permute-start | bytes 1769480 | tf_op jit(solution)/shard_map/ppermute | solution.py:569
  97.5 8.9 %collective-permute-start.21 = (bf16[16,2,128,128]{3,2,1,0:T(8,128)(2,1)S(1)}, bf16[16,2,128,128]{3,2,1,0:T(8,128)(2,1)S(1)}, u32[]{:S(2)}, u32[]{:S(2)}) collective-permute-start(bf16[16,2,128,128]{3,2,1,0:T(8,128)(2,1)S(1)} %get-tuple-element.50.env_ref), channel_id=1, source_target_pairs={{0,1},{2,3},{4,5},{6,7},{8,9},{10,11},{12,13},{14,15},{16,17},{18,... | collective-permute-start | bytes 3145736 | tf_op jit(solution)/shard_map/ppermute | solution.py:680
  98.8 12.5 %collective-permute-start.20 = (bf16[16,2,128,128]{3,2,1,0:T(8,128)(2,1)S(1)}, bf16[16,2,128,128]{3,2,1,0:T(8,128)(2,1)S(1)}, u32[]{:S(2)}, u32[]{:S(2)}) collective-permute-start(bf16[16,2,128,128]{3,2,1,0:T(8,128)(2,1)S(1)} %get-tuple-element.50.env_ref), channel_id=1, source_target_pairs={{1,8},{3,10},{5,12},{7,14},{9,24},{11,26},{13,28},{15,30},{17,0},{... | collective-permute-start | bytes 3145736 | tf_op jit(solution)/shard_map/ppermute | solution.py:677
  99.6 3.4 %collective-permute-start.9 = (bf16[18,128,128]{2,1,0:T(8,128)(2,1)S(1)}, bf16[18,128,128]{2,1,0:T(8,128)(2,1)S(1)}, u32[]{:S(2)}, u32[]{:S(2)}) collective-permute-start(bf16[18,128,128]{2,1,0:T(8,128)(2,1)S(1)} %collective-permute-done.8.refs_3_.refs_10_), channel_id=1, source_target_pairs={{0,1},{1,0},{2,3},{3,2},{4,5},{5,4},{6,7},{7,6},{8,9},{9,8},{10,11... | collective-permute-start | bytes 1769480 | tf_op jit(solution)/shard_map/ppermute | solution.py:576
  112.1 21.1 %collective-permute-start.23 = (bf16[16,2,128,128]{3,2,1,0:T(8,128)(2,1)S(1)}, bf16[16,2,128,128]{3,2,1,0:T(8,128)(2,1)S(1)}, u32[]{:S(2)}, u32[]{:S(2)}) collective-permute-start(bf16[16,2,128,128]{3,2,1,0:T(8,128)(2,1)S(1)} %get-tuple-element.51.env_ref), channel_id=1, source_target_pairs={{0,1},{2,3},{4,5},{6,7},{8,9},{10,11},{12,13},{14,15},{16,17},{18,... | collective-permute-start | bytes 3145736 | tf_op jit(solution)/shard_map/ppermute | solution.py:680
  113.4 24.1 %collective-permute-start.22 = (bf16[16,2,128,128]{3,2,1,0:T(8,128)(2,1)S(1)}, bf16[16,2,128,128]{3,2,1,0:T(8,128)(2,1)S(1)}, u32[]{:S(2)}, u32[]{:S(2)}) collective-permute-start(bf16[16,2,128,128]{3,2,1,0:T(8,128)(2,1)S(1)} %shard_map.76.refs_0_), channel_id=1, source_target_pairs={{1,8},{3,10},{5,12},{7,14},{9,24},{11,26},{13,28},{15,30},{17,0},{... | collective-permute-start | bytes 3145736 | tf_op jit(solution)/shard_map/ppermute | solution.py:677
  114.5 15.2 %collective-permute-start.10 = (bf16[6,128,128]{2,1,0:T(8,128)(2,1)S(1)}, bf16[6,128,128]{2,1,0:T(8,128)(2,1)S(1)}, u32[]{:S(2)}, u32[]{:S(2)}) collective-permute-start(bf16[6,128,128]{2,1,0:T(8,128)(2,1)S(1)} %shard_map.67), channel_id=1, source_target_pairs={{1,17},{3,19},{5,21},{7,23},{9,1},{11,3},{13,5},{15,7},{25,9},{27,... | collective-permute-start | bytes 589832 | tf_op jit(solution)/shard_map/ppermute | solution.py:611
  140.7 6.3 %collective-permute-start.24 = (bf16[4,2,128,128]{3,2,1,0:T(8,128)(2,1)S(1)}, bf16[4,2,128,128]{3,2,1,0:T(8,128)(2,1)S(1)}, u32[]{:S(2)}, u32[]{:S(2)}) collective-permute-start(bf16[4,2,128,128]{3,2,1,0:T(8,128)(2,1)S(1)} %shard_map.82), channel_id=1, source_target_pairs={{0,1},{2,3},{4,5},{6,7},{8,9},{10,11},{12,13},{14,15},{16,17},{18,... | collective-permute-start | bytes 786440 | tf_op jit(solution)/shard_map/ppermute | solution.py:729
  147.3 8.3 %collective-permute-start.25 = (bf16[2,2,128,128]{3,2,1,0:T(8,128)(2,1)S(1)}, bf16[2,2,128,128]{3,2,1,0:T(8,128)(2,1)S(1)}, u32[]{:S(2)}, u32[]{:S(2)}) collective-permute-start(bf16[2,2,128,128]{3,2,1,0:T(8,128)(2,1)S(1)} %get-tuple-element.58), channel_id=1, source_target_pairs={{0,1},{1,0},{2,3},{3,2},{4,5},{5,4},{6,7},{7,6},{8,9},{9,8},{10,11... | collective-permute-start | bytes 393224 | tf_op jit(solution)/shard_map/ppermute | solution.py:743
  152.1 5.0 %collective-permute-start.26 = (bf16[2,2,128,128]{3,2,1,0:T(8,128)(2,1)S(1)}, bf16[2,2,128,128]{3,2,1,0:T(8,128)(2,1)S(1)}, u32[]{:S(2)}, u32[]{:S(2)}) collective-permute-start(bf16[2,2,128,128]{3,2,1,0:T(8,128)(2,1)S(1)} %get-tuple-element.59), channel_id=1, source_target_pairs={{0,8},{1,9},{2,10},{3,11},{4,12},{5,13},{6,14},{7,15},{8,0},{9,1},... | collective-permute-start | bytes 393224 | tf_op jit(solution)/shard_map/ppermute | solution.py:743
  152.1 8.9 %collective-permute-start.27 = (bf16[2,2,128,128]{3,2,1,0:T(8,128)(2,1)S(1)}, bf16[2,2,128,128]{3,2,1,0:T(8,128)(2,1)S(1)}, u32[]{:S(2)}, u32[]{:S(2)}) collective-permute-start(bf16[2,2,128,128]{3,2,1,0:T(8,128)(2,1)S(1)} %get-tuple-element.60), channel_id=1, source_target_pairs={{0,9},{1,8},{2,11},{3,10},{4,13},{5,12},{6,15},{7,14},{8,1},{9,0},... | collective-permute-start | bytes 393224 | tf_op jit(solution)/shard_map/ppermute | solution.py:743
  153.8 7.2 %collective-permute-start.28 = (bf16[2,2,128,128]{3,2,1,0:T(8,128)(2,1)S(1)}, bf16[2,2,128,128]{3,2,1,0:T(8,128)(2,1)S(1)}, u32[]{:S(2)}, u32[]{:S(2)}) collective-permute-start(bf16[2,2,128,128]{3,2,1,0:T(8,128)(2,1)S(1)} %get-tuple-element.61), channel_id=1, source_target_pairs={{0,16},{1,17},{2,18},{3,19},{4,20},{5,21},{6,22},{7,23},{8,24},{9,... | collective-permute-start | bytes 393224 | tf_op jit(solution)/shard_map/ppermute | solution.py:743
  153.8 13.6 %collective-permute-start.29 = (bf16[2,2,128,128]{3,2,1,0:T(8,128)(2,1)S(1)}, bf16[2,2,128,128]{3,2,1,0:T(8,128)(2,1)S(1)}, u32[]{:S(2)}, u32[]{:S(2)}) collective-permute-start(bf16[2,2,128,128]{3,2,1,0:T(8,128)(2,1)S(1)} %get-tuple-element.62), channel_id=1, source_target_pairs={{0,17},{1,16},{2,19},{3,18},{4,21},{5,20},{6,23},{7,22},{8,25},{9,... | collective-permute-start | bytes 393224 | tf_op jit(solution)/shard_map/ppermute | solution.py:743
  155.6 11.9 %collective-permute-start.30 = (bf16[2,2,128,128]{3,2,1,0:T(8,128)(2,1)S(1)}, bf16[2,2,128,128]{3,2,1,0:T(8,128)(2,1)S(1)}, u32[]{:S(2)}, u32[]{:S(2)}) collective-permute-start(bf16[2,2,128,128]{3,2,1,0:T(8,128)(2,1)S(1)} %get-tuple-element.63), channel_id=1, source_target_pairs={{0,24},{1,25},{2,26},{3,27},{4,28},{5,29},{6,30},{7,31},{8,16},{9,... | collective-permute-start | bytes 393224 | tf_op jit(solution)/shard_map/ppermute | solution.py:743
  157.1 10.4 %collective-permute-start.31 = (bf16[2,2,128,128]{3,2,1,0:T(8,128)(2,1)S(1)}, bf16[2,2,128,128]{3,2,1,0:T(8,128)(2,1)S(1)}, u32[]{:S(2)}, u32[]{:S(2)}) collective-permute-start(bf16[2,2,128,128]{3,2,1,0:T(8,128)(2,1)S(1)} %get-tuple-element.64), channel_id=1, source_target_pairs={{0,25},{1,24},{2,27},{3,26},{4,29},{5,28},{6,31},{7,30},{8,17},{9,... | collective-permute-start | bytes 393224 | tf_op jit(solution)/shard_map/ppermute | solution.py:743
  (22 other events, 279.3 us)
